TPU v7x, 512 devices: a whole 4x8x8 slice. The times are simulated.
512 devices in a mesh: expert: 8 (over y), tensor: 64 (over z, x, core).
Axes of the slice: x: 4, y: 8, z: 8, core: 2. Of those that a mesh axis runs over, the one named last changes fastest.
Arguments:
- expert_hidden: bfloat16 [8, 768, 8192], P('expert', 'tensor'), may hold values from -6 to 6
- probe_tangent: bfloat16 [8, 6144, 8192], P('expert', 'tensor'), may hold values from -0.0625 to 0.0625
- routed_experts: int32 [1536, 2], P('expert'), may hold values from 0 to 7, all different within a row; in each aligned block of 192 rows (0 to 191, 192 to 383, ...) at most 96 rows name the same one
- gate_weights: float32 [1536, 2], P('expert'), may hold values from 0.1 to 1
Outputs:
- ggn_product: bfloat16 [8, 6144, 8192], P('expert', 'tensor')
- token_quadratic: float32 [1536], P('expert')
Inputs may be any that keep to these rules, and one draw needn't show every extreme that they name: `routed_experts`: each row names two different experts. Among the 192 rows of one source, no expert is named by more than 96 rows, a bound that some block reaches.
All inputs are finite; a program needn't handle non-finite values.
Results may differ from a plain program's by a relative error of at most 0.0057.
Values may be sent and summed in bfloat16 or wider, within the bound.
No kernel may reach another device: no remote copies, remote signals or barrier semaphores. Data moves between devices by JAX's collectives and lax.ppermute only.
A program may use at most 128 MiB of HBM per device.

v0:
```python
import jax
import jax.numpy as jnp
from jax import lax
from jax.sharding import PartitionSpec as P


def local(expert_hidden, probe_tangent, routed_experts, gate_weights):
    expert_count = lax.axis_size("expert")
    tensor_count = lax.axis_size("tensor")
    hidden_local = expert_hidden[0]
    probe_local = probe_tangent[0]
    col_count = probe_local.shape[0]
    tok_count = routed_experts.shape[0]
    capacity = hidden_local.shape[0] * tensor_count // expert_count
    ids_flat = routed_experts.reshape(-1)
    gate_flat = gate_weights.reshape(-1)
    one_hot = (ids_flat[:, None] == jnp.arange(expert_count, dtype=jnp.int32)[None, :]).astype(
        jnp.int32
    )
    earlier = jnp.cumsum(one_hot, axis=0) - one_hot
    slot_rank = jnp.sum(one_hot * earlier, axis=1)
    buffer_row = ids_flat * capacity + slot_rank
    hidden_all = lax.all_gather(hidden_local, "tensor", axis=0, tiled=True)
    expert_tangent = lax.dot_general(
        hidden_all, probe_local, (((1,), (1,)), ((), ())), preferred_element_type=jnp.float32
    ).astype(jnp.bfloat16)
    outgoing = expert_tangent.reshape(expert_count, capacity, col_count)
    received = lax.all_to_all(outgoing, "expert", split_axis=0, concat_axis=0, tiled=True)
    block_cols = received.shape[2]
    flat_rows = received.reshape(expert_count * capacity, block_cols)
    picked = flat_rows[buffer_row].astype(jnp.float32) * gate_flat[:, None]
    token_tangent = jnp.sum(picked.reshape(tok_count, 2, block_cols), axis=1)
    weighted = (token_tangent[:, None, :] * gate_weights[:, :, None]).reshape(
        tok_count * 2, block_cols
    )
    weighted = weighted.astype(jnp.bfloat16)
    buffer = (
        jnp.zeros((expert_count * capacity, block_cols), jnp.bfloat16).at[buffer_row].set(weighted)
    )
    buffer, token_tangent = (buffer, token_tangent)
    returning = lax.all_to_all(
        buffer.reshape(expert_count, capacity, col_count),
        "expert",
        split_axis=0,
        concat_axis=0,
        tiled=True,
    )
    returning_flat = returning.reshape(expert_count * capacity, col_count)
    gradient = lax.dot_general(
        returning_flat, hidden_all, (((0,), (0,)), ((), ())), preferred_element_type=jnp.float32
    ).astype(jnp.bfloat16)
    partial_squares = jnp.sum(token_tangent * token_tangent, axis=1)
    total_squares = lax.psum(partial_squares, "tensor")
    token_quadratic = total_squares / (col_count * tensor_count)
    return (gradient[None], token_quadratic)


def solution(mesh):
    placed = (
        P("expert", "tensor", None),
        P("expert", "tensor", None),
        P("expert", None),
        P("expert", None),
    )
    return jax.shard_map(
        local,
        mesh=mesh,
        in_specs=placed,
        out_specs=(P("expert", "tensor", None), P("expert")),
        check_vma=False,
    )
```

profile of v0, /device:TPU:1, one launch (start us, length us, event | category | flops | bytes accessed | tf_op | source)
XLA Modules:
  0.0 347.5 jit_solution(15207525154912715444)
XLA Ops:
  7.2 0.0 copy-start
  7.2 0.0 all-gather.3.cloned.1.call-start
  7.2 2.1 copy.33
  9.4 0.0 all-gather.3.cloned.1.call-update
  9.4 0.8 copy.31
  10.2 0.1 eq.29
  10.3 0.1 eq.25
  10.5 0.9 reduce-window.6
  11.4 0.2 slice_reduce_fusion
  11.6 0.7 broadcast_multiply_fusion
  12.3 132.1 %all-gather.3.cloned.1.call-done = bf16[1,768,8192]{2,0,1:T(2,128)(2,1)} async-done(((bf16[1,12,8192]{2,0,1:T(2,128)(2,1)}), bf16[1,768,8192]{2,0,1:T(2,128)(2,1)}) %all-gather.3.cloned.1.call-update) | async-done | bytes 12582928 | tf_op jit(solution)/shard_map/all_gather | solution.py:23
  144.4 22.4 %fusion.13 = bf16[768,96]{0,1:T(8,128)(2,1)S(1)} fusion(bf16[1,96,8192]{2,1,0:T(8,128)(2,1)S(1)} %copy-done, bf16[1,768,8192]{2,0,1:T(2,128)(2,1)} %all-gather.3.cloned.1.call-done), kind=kOutput, calls=%fused_computation.11 | convolution fusion | flops 1208033280 | bytes 14303232 | tf_op jit(solution)/shard_map/dot_general | solution.py:24
  166.8 0.2 reshape.79
  167.0 0.7 copy.34
  167.7 6.5 %all-to-all-start = ((bf16[8,96,96]{1,2,0:T(8,128)(2,1)}), bf16[8,96,96]{1,2,0:T(8,128)(2,1)S(1)}, u32[]{:S(2)}, u32[]{:S(2)}) async-start(bf16[8,96,96]{1,2,0:T(8,128)(2,1)} %copy.34), calls=%async_computation | async-start | bytes 393216 | tf_op jit(solution)/shard_map/all_to_all | solution.py:28
  174.2 0.1 fusion.23
  174.3 0.1 copy.30
  174.4 0.1 mul.51
  174.6 0.1 copy.36
  174.7 0.1 mul.57
  174.9 8.9 %all-to-all-done = bf16[8,96,96]{1,2,0:T(8,128)(2,1)S(1)} async-done(((bf16[8,96,96]{1,2,0:T(8,128)(2,1)}), bf16[8,96,96]{1,2,0:T(8,128)(2,1)S(1)}, u32[]{:S(2)}, u32[]{:S(2)}) %all-to-all-start) | async-done | bytes 147488 | tf_op jit(solution)/shard_map/all_to_all | solution.py:28
  183.8 0.1 copy.35
  183.9 1.4 gather_fusion
  185.4 0.3 fusion.18
  185.7 0.1 mul.55
  185.8 2.2 scatter_custom_fusion
  188.0 3.4 all-to-all-start.1
  191.4 0.1 multiply_reduce_fusion
  191.5 125.3 %psum.7 = f32[192]{0:T(256)S(1)} all-reduce(f32[192]{0:T(256)S(1)} %multiply_reduce_fusion), channel_id=1, replica_groups=mesh['expert'=8,'tensor'=64] {'tensor'}, use_global_device_ids=true, to_apply=%region_6.7 | all-reduce | flops 192 | bytes 1536 | tf_op jit(solution)/shard_map/psum | solution.py:53
  316.8 0.6 broadcast_multiply_fusion.1
  317.3 0.0 all-to-all-done.1
  317.3 23.3 %fusion.7 = bf16[1,96,8192]{2,1,0:T(8,128)(2,1)} fusion(bf16[768,96]{1,0:T(8,128)(2,1)S(1)} %bitcast.38, bf16[1,768,8192]{2,0,1:T(2,128)(2,1)} %all-gather.3.cloned.1.call-done), kind=kOutput, calls=%fused_computation.7 | convolution fusion | flops 1208745984 | bytes 14303232 | tf_op jit(solution)/shard_map/dot_general | solution.py:49
  (7 shorter events, 0.1 us)
Async XLA Ops:
  7.2 137.2 %copy-start = (bf16[1,96,8192]{2,1,0:T(8,128)(2,1)S(1)}, bf16[1,96,8192]{2,1,0:T(8,128)(2,1)}, u32[]{:S(2)}) copy-start(bf16[1,96,8192]{2,1,0:T(8,128)(2,1)} %param.5) | copy-start | bytes 4718596
  7.2 167.4 %copy-start.1 = (f32[192,2]{0,1:T(2,128)S(1)}, f32[192,2]{0,1:T(2,128)}, u32[]{:S(2)}) copy-start(f32[192,2]{0,1:T(2,128)} %param.7) | copy-start | bytes 4612
  7.2 137.2 %all-gather.3.cloned.1.call-start = ((), (), s32[]{:S(2)}) async-start(), calls=%async_computation.2 | async-start | bytes 25559040 | tf_op jit(solution)/shard_map/all_gather | solution.py:23
  167.7 16.0 %all-to-all-start = ((bf16[8,96,96]{1,2,0:T(8,128)(2,1)}), bf16[8,96,96]{1,2,0:T(8,128)(2,1)S(1)}, u32[]{:S(2)}, u32[]{:S(2)}) async-start(bf16[8,96,96]{1,2,0:T(8,128)(2,1)} %copy.34), calls=%async_computation | async-start | bytes 393216 | tf_op jit(solution)/shard_map/all_to_all | solution.py:28
  188.0 129.3 %all-to-all-start.1 = ((bf16[8,96,96]{2,1,0:T(8,128)(2,1)}), bf16[8,96,96]{2,1,0:T(8,128)(2,1)S(1)}, u32[]{:S(2)}, u32[]{:S(2)}) async-start(bf16[8,96,96]{2,1,0:T(8,128)(2,1)} %bitcast.6), calls=%async_computation.1 | async-start | bytes 393216 | tf_op jit(solution)/shard_map/all_to_all | solution.py:41
Sparse Core Ops, SparseCore 0:
  11.9 132.4 all-gather.2
where the time goes:
time: 348 us
  waiting for transfers between devices  141 us (41%)
  blocking collectives  125 us (36%)
  matrix products  45.7 us (13%)
  between operations  14.2 us (4%)
  starting transfers between devices  9.89 us (3%)
  local copies, waits for them, and re-layouts  6.58 us (2%)
  other arithmetic  4.95 us (1%)
    all_gather x1, waiting for transfers between devices, local(): hidden_all = lax.all_gather(hidden_local, 'tensor', axis=0, tiled=True)  132 us
    psum x1, blocking collectives, local(): total_squares = lax.psum(partial_squares, 'tensor')  125 us
    dot_general x1, matrix products, local(): lax.dot_general(returning_flat, hidden_all, (((0,), (0,)), ((), ())), pre...  23.3 us
    dot_general x1, matrix products, local(): lax.dot_general(hidden_all, probe_local, (((1,), (1,)), ((), ())), prefer...  22.4 us
    all_to_all x1, waiting for transfers between devices, local(): lax.all_to_all(outgoing, 'expert', split_axis=0, concat_axis=0, tiled=True)  8.9 us
  transfers between devices with their start and end apart: 3, of which 2 were waited for; matrix products, arithmetic and copies ran while one was open for 1% of the time, Pallas kernels for 0%

commit v1 on v0

v1 whole, which is shorter than its diff:
```python
import jax
import jax.numpy as jnp
from jax import lax
from jax.experimental import pallas as pl
from jax.experimental.pallas import tpu as pltpu
from jax.sharding import Mesh, PartitionSpec as P


LANES = 128


def forward_kernel(x_ref, p_ref, o_ref, pc_ref, y0_ref, y1_ref):
    cols, half = p_ref.shape[0], x_ref.shape[1]
    rows = o_ref.shape[0]

    @pl.when(pl.program_id(0) == 0)
    def _():
        pc_ref[...] = jnp.zeros_like(pc_ref)
        pc_ref[0:cols, :] = p_ref[:, 0:half]
        pc_ref[LANES : LANES + cols, :] = p_ref[:, half : 2 * half]

    y = lax.dot_general(
        x_ref[...], pc_ref[...], (((1,), (1,)), ((), ())), preferred_element_type=jnp.float32
    )
    y0_ref[...] = y[:, 0:LANES]
    y1_ref[...] = y[:, LANES : 2 * LANES]
    total = y0_ref[pl.ds(0, rows, stride=2), :] + y1_ref[pl.ds(1, rows, stride=2), :]
    o_ref[...] = total.astype(o_ref.dtype)


def forward(x, probe, block=384):
    rows, half = x.shape
    cols = probe.shape[0]
    return pl.pallas_call(
        forward_kernel,
        grid=(rows // block,),
        in_specs=[
            pl.BlockSpec((block, half), lambda i: (i, 0)),
            pl.BlockSpec((cols, 2 * half), lambda i: (0, 0)),
        ],
        out_specs=pl.BlockSpec((block // 2, LANES), lambda i: (i, 0)),
        out_shape=jax.ShapeDtypeStruct((rows // 2, LANES), jnp.bfloat16),
        scratch_shapes=[
            pltpu.VMEM((2 * LANES, half), jnp.bfloat16),
            pltpu.VMEM((block, LANES), jnp.float32),
            pltpu.VMEM((block, LANES), jnp.float32),
        ],
    )(x, probe)


def combine_kernel(t_ref, row_ref, gate_ref, b_ref, q_ref):
    rows = t_ref.shape[0]
    toks = row_ref.shape[0]
    lane = lax.broadcasted_iota(jnp.int32, (toks, rows), 1)
    zero = jnp.zeros((toks, rows), jnp.bfloat16)
    one = jnp.ones((toks, rows), jnp.bfloat16)
    total = None
    picks = []
    for k in range(2):
        pick = jnp.where(lane == row_ref[:, k : k + 1], one, zero)
        part = jnp.dot(pick, t_ref[...], preferred_element_type=jnp.float32)
        part = part * gate_ref[:, k : k + 1]
        total = part if total is None else total + part
        picks.append(pick)
    back = None
    for k in range(2):
        weighted = (total * gate_ref[:, k : k + 1]).astype(jnp.bfloat16)
        placed = lax.dot_general(
            picks[k], weighted, (((0,), (0,)), ((), ())), preferred_element_type=jnp.float32
        )
        back = placed if back is None else back + placed
    b_ref[...] = back.astype(b_ref.dtype)
    squares = jnp.sum(total * total, axis=1, keepdims=True)
    q_ref[...] = jnp.broadcast_to(squares, (toks, LANES)).T[0:8]


def combine(tangent, row, gate):
    rows = tangent.shape[0]
    toks = row.shape[0]
    return pl.pallas_call(
        combine_kernel,
        out_shape=(
            jax.ShapeDtypeStruct((rows, LANES), jnp.bfloat16),
            jax.ShapeDtypeStruct((8, toks), jnp.float32),
        ),
    )(tangent, row, gate)


def backward_kernel(r_ref, x_ref, o_ref, e_ref, f_ref, rt_ref, g_ref, sem):
    cols, half = o_ref.shape[0], o_ref.shape[1] // 2
    rows = r_ref.shape[0]
    block = x_ref.shape[1]
    step = pl.program_id(0)
    steps = pl.num_programs(0)

    @pl.when(step == 0)
    def _():
        rf = r_ref[...].astype(jnp.float32)
        zero = jnp.zeros_like(rf)
        e_ref[pl.ds(0, rows, stride=2), :] = rf
        e_ref[pl.ds(1, rows, stride=2), :] = zero
        f_ref[pl.ds(0, rows, stride=2), :] = zero
        f_ref[pl.ds(1, rows, stride=2), :] = rf
        rt_ref[0:cols, :] = e_ref[...].T.astype(jnp.bfloat16)[0:cols]
        rt_ref[cols : 2 * cols, :] = f_ref[...].T.astype(jnp.bfloat16)[0:cols]

    def copies(at):
        slot = lax.rem(at, 2)
        return [
            pltpu.make_async_copy(
                g_ref.at[slot, pl.ds(h * cols, cols), :],
                o_ref.at[:, pl.ds(pl.multiple_of(h * half + at * block, block), block)],
                sem.at[slot, h],
            )
            for h in range(2)
        ]

    @pl.when(step >= 2)
    def _():
        for copy in copies(step - 2):
            copy.wait()

    g = jnp.dot(rt_ref[...], x_ref[...], preferred_element_type=jnp.float32)
    g_ref[lax.rem(step, 2)] = g.astype(g_ref.dtype)
    for copy in copies(step):
        copy.start()

    @pl.when(step == steps - 1)
    def _():
        for copy in copies(step - 1) + copies(step):
            copy.wait()


def backward(returned, x, cols, block=1024):
    rows, half = x.shape
    return pl.pallas_call(
        backward_kernel,
        grid=(half // block,),
        in_specs=[
            pl.BlockSpec((rows // 2, LANES), lambda j: (0, 0)),
            pl.BlockSpec((rows, block), lambda j: (0, j)),
        ],
        out_specs=pl.BlockSpec(memory_space=pl.ANY),
        out_shape=jax.ShapeDtypeStruct((cols, 2 * half), jnp.bfloat16),
        scratch_shapes=[
            pltpu.VMEM((rows, LANES), jnp.float32),
            pltpu.VMEM((rows, LANES), jnp.float32),
            pltpu.VMEM((2 * cols, rows), jnp.bfloat16),
            pltpu.VMEM((2, 2 * cols, block), jnp.bfloat16),
            pltpu.SemaphoreType.DMA((2, 2)),
        ],
    )(returned, x)


def local(expert_hidden, probe_tangent, routed_experts, gate_weights):
    tensor = ("z", "x", "c")
    experts = lax.axis_size("expert")
    parts = lax.axis_size(tensor)
    hidden = expert_hidden[0]
    probe = probe_tangent[0]
    cols = probe.shape[0]
    toks = routed_experts.shape[0]
    capacity = hidden.shape[0] * parts // experts

    x_own = hidden.reshape(2 * hidden.shape[0], hidden.shape[1] // 2)
    x = lax.all_gather(x_own, tensor, axis=0, tiled=True)

    ids = routed_experts.reshape(-1)
    one_hot = (ids[:, None] == jnp.arange(experts, dtype=jnp.int32)[None, :]).astype(jnp.int32)
    earlier = jnp.cumsum(one_hot, axis=0) - one_hot
    rank = jnp.sum(one_hot * earlier, axis=1)
    row = (ids * capacity + rank).reshape(toks, 2)

    tangent = forward(x, probe)
    tangent = lax.all_to_all(
        tangent.reshape(experts, capacity, LANES), "expert", split_axis=0, concat_axis=0, tiled=True
    )
    back, squares = combine(tangent.reshape(experts * capacity, LANES), row, gate_weights)
    back = lax.all_to_all(
        back.reshape(experts, capacity, LANES),
        "expert",
        split_axis=0,
        concat_axis=0,
        tiled=True,
    )
    shares = jnp.broadcast_to(squares[0:1][None], (parts, 1, toks))
    shares = lax.all_to_all(shares, tensor, split_axis=0, concat_axis=0, tiled=True)
    gradient = backward(back.reshape(experts * capacity, LANES), x, cols)
    quadratic = jnp.sum(shares, axis=(0, 1)) / (cols * parts)
    return gradient[None], quadratic


def solution(mesh):
    grid = Mesh(mesh.devices.reshape(8, 8, 4, 2), ("expert", "z", "x", "c"))
    tensor = ("z", "x", "c")
    return jax.shard_map(
        local,
        mesh=grid,
        in_specs=(
            P("expert", tensor, None),
            P("expert", tensor, None),
            P("expert", None),
            P("expert", None),
        ),
        out_specs=(P("expert", tensor, None), P("expert")),
        check_vma=False,
    )
```

time: 348 us -> 188 us (0.54)
  blocking collectives: 125 us -> 17.3 us
  matrix products: 45.7 us -> 0 us
  waiting for transfers between devices: 141 us -> 118 us
  Pallas kernels: 0 us -> 18.8 us
    psum x1 -> x0, blocking collectives: 125 us -> none  [local(): total_squares = lax.psum(partial_squares, 'tensor')]
    dot_general x2 -> x0, matrix products: 45.7 us -> none  [the longest x1 23.3 us: local(): lax.dot_general(returning_flat, hidden_all, (((0,), (0,)), ((), ())), pre...]
    all_gather x1, waiting for transfers between devices: 132 us -> 102 us  [local(): x = lax.all_gather(x_own, tensor, axis=0, tiled=True)]
    pallas_call x0 -> x3, Pallas kernels: none -> 18.8 us  [the longest x1 8.42 us: forward(): pl.pallas_call(forward_kernel, grid=(rows // block,), in_specs=[pl.BlockS...]
    all_to_all x0 -> x1, blocking collectives: none -> 17.3 us  [local(): lax.all_to_all(shares, tensor, split_axis=0, concat_axis=0, tiled=True)]
    all_to_all x2, waiting for transfers between devices: 8.91 us -> 16 us  [the longest x1 9.19 us: local(): lax.all_to_all(back.reshape(experts, capacity, LANES), 'expert', split_ax...]
  transfers between devices with their start and end apart: 3 -> 3, of which waited for: 2 -> 3; matrix products, arithmetic and copies ran while one was open for 1% -> 3% of each run, Pallas kernels for 0% -> 0%
where the time goes in v1:
time: 188 us
  waiting for transfers between devices  118 us (63%)
  Pallas kernels  18.8 us (10%)
  blocking collectives  17.3 us (9%)
  between operations  14.1 us (8%)
  starting transfers between devices  9.89 us (5%)
  local copies, waits for them, and re-layouts  6.12 us (3%)
  other arithmetic  3 us (2%)
    all_gather x1, waiting for transfers between devices, local(): x = lax.all_gather(x_own, tensor, axis=0, tiled=True)  102 us
    all_to_all x1, blocking collectives, local(): lax.all_to_all(shares, tensor, split_axis=0, concat_axis=0, tiled=True)  17.3 us
    all_to_all x1, waiting for transfers between devices, local(): lax.all_to_all(back.reshape(experts, capacity, LANES), 'expert', split_ax...  9.19 us
    pallas_call x1, Pallas kernels, forward(): pl.pallas_call(forward_kernel, grid=(rows // block,), in_specs=[pl.BlockS...  8.42 us
    pallas_call x1, Pallas kernels, backward(): pl.pallas_call(backward_kernel, grid=(half // block,), in_specs=[pl.Block...  7.87 us
    all_to_all x1, waiting for transfers between devices, local(): lax.all_to_all(tangent.reshape(experts, capacity, LANES), 'expert', split...  6.79 us
    all_to_all x1, starting transfers between devices, local(): lax.all_to_all(tangent.reshape(experts, capacity, LANES), 'expert', split...  6.46 us
  transfers between devices with their start and end apart: 3, of which 3 were waited for; matrix products, arithmetic and copies ran while one was open for 3% of the time, Pallas kernels for 0%

profile of v1, /device:TPU:1, one launch (start us, length us, event | category | flops | bytes accessed | tf_op | source)
XLA Modules:
  0.0 187.7 jit_solution(8816678424619711575)
XLA Ops:
  7.2 0.0 all-gather.2.cloned.1.call-start
  7.2 1.7 reshape_squeeze.3
  8.9 0.0 all-gather.2.cloned.1.call-update
  8.9 0.8 copy.25
  9.7 0.1 eq.29
  9.9 0.1 eq.25
  10.0 0.7 broadcast_multiply_fusion
  10.7 0.1 copy.27
  10.8 102.5 %all-gather.2.cloned.1.call-done.x_ref = bf16[1536,4096]{1,0:T(8,128)(2,1)} async-done(((bf16[24,4096]{1,0:T(8,128)(2,1)}), bf16[1536,4096]{1,0:T(8,128)(2,1)}) %all-gather.2.cloned.1.call-update) | async-done | bytes 12582928 | tf_op jit(solution)/shard_map/all_gather | solution.py:166
  113.3 0.0 copy-start.2
  113.3 8.4 %shard_map.59 = bf16[768,128]{1,0:T(8,128)(2,1)} custom-call(bf16[1536,4096]{1,0:T(8,128)(2,1)} %all-gather.2.cloned.1.call-done.x_ref, bf16[96,8192]{1,0:T(8,128)(2,1)} %bitcast.16), custom_call_target="tpu_custom_call" | custom-call | tf_op jit(solution)/shard_map/pallas_call | solution.py:34
  121.7 6.5 %all-to-all-start = ((bf16[8,96,128]{2,1,0:T(8,128)(2,1)}), bf16[8,96,128]{2,1,0:T(8,128)(2,1)S(1)}, u32[]{:S(2)}, u32[]{:S(2)}) async-start(bf16[8,96,128]{2,1,0:T(8,128)(2,1)} %bitcast.18), calls=%async_computation | async-start | bytes 393216 | tf_op jit(solution)/shard_map/all_to_all | solution.py:175
  128.2 0.9 reduce-window.6
  129.1 0.2 slice_reduce_fusion
  129.3 0.1 fusion.1
  129.4 0.1 reduce_sum.21
  129.6 0.0 copy-done.2
  129.6 0.8 copy.28.gate_ref
  130.4 0.6 add.4.row_ref
  131.0 6.8 %all-to-all-done = bf16[8,96,128]{2,1,0:T(8,128)(2,1)S(1)} async-done(((bf16[8,96,128]{2,1,0:T(8,128)(2,1)}), bf16[8,96,128]{2,1,0:T(8,128)(2,1)S(1)}, u32[]{:S(2)}, u32[]{:S(2)}) %all-to-all-start) | async-done | bytes 196640 | tf_op jit(solution)/shard_map/all_to_all | solution.py:175
  137.8 0.0 copy-start.1
  137.8 0.7 copy-done.1
  138.5 2.5 %shard_map.60 = (bf16[768,128]{1,0:T(8,128)(2,1)}, f32[8,192]{1,0:T(8,128)}) custom-call(bf16[768,128]{1,0:T(8,128)(2,1)} %bitcast.20, s32[192,2]{1,0:T(8,128)} %add.4.row_ref, f32[192,2]{1,0:T(8,128)} %copy.28.gate_ref), custom_call_target="tpu_custom_call" | custom-call | tf_op jit(solution)/shard_map/pallas_call | solution.py:80
  141.0 0.7 slice.11
  141.7 17.3 %all_to_all.15 = f32[64,1,192]{2,1,0:T(1,128)S(1)} all-to-all(f32[64,1,192]{2,1,0:T(1,128)S(1)} %broadcast_in_dim.14), channel_id=1, replica_groups=mesh['expert'=8,'z'=8,'x'=4,'c'=2] {'z','x','c'}, dimensions={0} | all-to-all | bytes 98304 | tf_op jit(solution)/shard_map/all_to_all | solution.py:187
  159.0 3.4 %all-to-all-start.1 = ((bf16[8,96,128]{2,1,0:T(8,128)(2,1)}), bf16[8,96,128]{2,1,0:T(8,128)(2,1)S(1)}, u32[]{:S(2)}, u32[]{:S(2)}) async-start(bf16[8,96,128]{2,1,0:T(8,128)(2,1)} %bitcast.21), calls=%async_computation.1 | async-start | bytes 393216 | tf_op jit(solution)/shard_map/all_to_all | solution.py:179
  162.4 0.1 reduce_sum.22
  162.5 0.6 broadcast_multiply_fusion.1
  163.1 9.2 %all-to-all-done.1 = bf16[8,96,128]{2,1,0:T(8,128)(2,1)S(1)} async-done(((bf16[8,96,128]{2,1,0:T(8,128)(2,1)}), bf16[8,96,128]{2,1,0:T(8,128)(2,1)S(1)}, u32[]{:S(2)}, u32[]{:S(2)}) %all-to-all-start.1) | async-done | bytes 196640 | tf_op jit(solution)/shard_map/all_to_all | solution.py:179
  172.2 0.0 copy-start
  172.2 0.7 copy-done
  172.9 7.9 %shard_map.61 = bf16[96,8192]{1,0:T(8,128)(2,1)} custom-call(bf16[768,128]{1,0:T(8,128)(2,1)} %bitcast.19, bf16[1536,4096]{1,0:T(8,128)(2,1)} %all-gather.2.cloned.1.call-done.x_ref), custom_call_target="tpu_custom_call" | custom-call | tf_op jit(solution)/shard_map/pallas_call | solution.py:136
  (3 shorter events, 0.1 us)
Async XLA Ops:
  7.2 106.2 %all-gather.2.cloned.1.call-start = ((), (), s32[]{:S(2)}) async-start(), calls=%async_computation.3 | async-start | bytes 12779520 | tf_op jit(solution)/shard_map/all_gather | solution.py:166
  113.3 16.3 %copy-start.2 = (f32[192,2]{0,1:T(2,128)S(1)}, f32[192,2]{0,1:T(2,128)}, u32[]{:S(2)}) copy-start(f32[192,2]{0,1:T(2,128)} %param.7) | copy-start | bytes 4612
  121.7 16.0 %all-to-all-start = ((bf16[8,96,128]{2,1,0:T(8,128)(2,1)}), bf16[8,96,128]{2,1,0:T(8,128)(2,1)S(1)}, u32[]{:S(2)}, u32[]{:S(2)}) async-start(bf16[8,96,128]{2,1,0:T(8,128)(2,1)} %bitcast.18), calls=%async_computation | async-start | bytes 393216 | tf_op jit(solution)/shard_map/all_to_all | solution.py:175
  137.8 0.7 copy-start.1
  159.0 13.3 %all-to-all-start.1 = ((bf16[8,96,128]{2,1,0:T(8,128)(2,1)}), bf16[8,96,128]{2,1,0:T(8,128)(2,1)S(1)}, u32[]{:S(2)}, u32[]{:S(2)}) async-start(bf16[8,96,128]{2,1,0:T(8,128)(2,1)} %bitcast.21), calls=%async_computation.1 | async-start | bytes 393216 | tf_op jit(solution)/shard_map/all_to_all | solution.py:179
  172.2 0.7 copy-start
Sparse Core Ops, SparseCore 0:
  11.9 101.3 all-gather.1

commit v2 on v1

v2 whole, which is shorter than its diff:
```python
import functools

import jax
import jax.numpy as jnp
from jax import lax
from jax.experimental import pallas as pl
from jax.experimental.pallas import tpu as pltpu
from jax.sharding import Mesh, PartitionSpec as P


LANES = 128
WIDTH_A, BLOCKS_A, BLOCKS_B = 1792, 2, 2


def stack_probe(pc_ref, p_ref, start):
    cols, half, width = p_ref.shape[0], p_ref.shape[1] // 2, pc_ref.shape[1]
    pc_ref[...] = jnp.zeros_like(pc_ref)
    pc_ref[0:cols, :] = p_ref[:, start : start + width]
    pc_ref[LANES : LANES + cols, :] = p_ref[:, half + start : half + start + width]


def times(x, y):
    return lax.dot_general(x, y, (((1,), (1,)), ((), ())), preferred_element_type=jnp.float32)


def places(at_ref):
    xs, x, core = 4, at_ref[0], at_ref[1]
    step = 1 - 2 * core
    behind = lax.rem(x - step + xs, xs)
    ahead = lax.rem(x + step + xs, xs)
    across = lax.rem(x + 2, xs)
    return [(x, 0), (behind, 0), (ahead, 0), (across, 4 * core), (across, 4 - 4 * core)]


def forward_b_kernel(start, at_ref, own, near, far, half0, half1, p_ref, y_ref, pc_ref):
    stack_probe(pc_ref, p_ref, start)
    for piece, (x, z) in zip((own, near, far, half0, half1), places(at_ref)):
        zs = piece.shape[0] // 48
        part = times(piece[...], pc_ref[...])
        y_ref[pl.ds(z, zs), :, pl.ds(x, 1)] = part.reshape(zs, 2, 1, 24, 2 * LANES)


def forward_b(at, pieces, probe, start):
    width = pieces[0].shape[1]
    rows = sum(p.shape[0] for p in pieces)
    vmem = pl.BlockSpec(memory_space=pltpu.VMEM)
    return pl.pallas_call(
        functools.partial(forward_b_kernel, start),
        in_specs=[pl.BlockSpec(memory_space=pltpu.SMEM)] + [vmem] * 6,
        out_specs=vmem,
        out_shape=jax.ShapeDtypeStruct((8, 2, 4, 24, 2 * LANES), jnp.float32),
        scratch_shapes=[pltpu.VMEM((2 * LANES, width), jnp.bfloat16)],
        cost_estimate=pl.CostEstimate(
            flops=2 * rows * width * 2 * LANES,
            bytes_accessed=2 * rows * width + 4 * rows * 2 * LANES,
            transcendentals=0,
        ),
    )(at, *pieces, probe)


def forward_a_kernel(x_ref, p_ref, yb_ref, o_ref, pc_ref, y0_ref, y1_ref):
    rows = o_ref.shape[0]

    @pl.when(pl.program_id(0) == 0)
    def _():
        stack_probe(pc_ref, p_ref, 0)

    y = times(x_ref[...], pc_ref[...]) + yb_ref[...]
    y0_ref[...] = y[:, 0:LANES]
    y1_ref[...] = y[:, LANES : 2 * LANES]
    total = y0_ref[pl.ds(0, rows, stride=2), :] + y1_ref[pl.ds(1, rows, stride=2), :]
    o_ref[...] = total.astype(o_ref.dtype)


def forward_a(x, probe, partial, block=384):
    rows, width = x.shape
    return pl.pallas_call(
        forward_a_kernel,
        grid=(rows // block,),
        in_specs=[
            pl.BlockSpec((block, width), lambda i: (i, 0)),
            pl.BlockSpec(probe.shape, lambda i: (0, 0)),
            pl.BlockSpec((block, 2 * LANES), lambda i: (i, 0)),
        ],
        out_specs=pl.BlockSpec((block // 2, LANES), lambda i: (i, 0)),
        out_shape=jax.ShapeDtypeStruct((rows // 2, LANES), jnp.bfloat16),
        scratch_shapes=[
            pltpu.VMEM((2 * LANES, width), jnp.bfloat16),
            pltpu.VMEM((block, LANES), jnp.float32),
            pltpu.VMEM((block, LANES), jnp.float32),
        ],
    )(x, probe, partial)


def combine_kernel(t_ref, row_ref, gate_ref, b_ref, q_ref):
    rows = t_ref.shape[0]
    toks = row_ref.shape[0]
    lane = lax.broadcasted_iota(jnp.int32, (toks, rows), 1)
    zero = jnp.zeros((toks, rows), jnp.bfloat16)
    one = jnp.ones((toks, rows), jnp.bfloat16)
    total = None
    picks = []
    for k in range(2):
        pick = jnp.where(lane == row_ref[:, k : k + 1], one, zero)
        part = jnp.dot(pick, t_ref[...], preferred_element_type=jnp.float32)
        part = part * gate_ref[:, k : k + 1]
        total = part if total is None else total + part
        picks.append(pick)
    back = None
    for k in range(2):
        weighted = (total * gate_ref[:, k : k + 1]).astype(jnp.bfloat16)
        placed = lax.dot_general(
            picks[k], weighted, (((0,), (0,)), ((), ())), preferred_element_type=jnp.float32
        )
        back = placed if back is None else back + placed
    b_ref[...] = back.astype(b_ref.dtype)
    squares = jnp.sum(total * total, axis=1, keepdims=True)
    q_ref[...] = jnp.broadcast_to(squares, (toks, LANES)).T[0:8]


def combine(tangent, row, gate):
    rows = tangent.shape[0]
    toks = row.shape[0]
    return pl.pallas_call(
        combine_kernel,
        out_shape=(
            jax.ShapeDtypeStruct((rows, LANES), jnp.bfloat16),
            jax.ShapeDtypeStruct((8, toks), jnp.float32),
        ),
    )(tangent, row, gate)


def backward_kernel(
    blocks, at_ref, r_ref, a_ref, own, near, far, half0, half1,
    o_ref, e_ref, f_ref, rt_ref, *rest,
):
    rb_refs, (ga_ref, gb_ref, sem) = rest[:5], rest[5:]
    (n_a, w_a), (n_b, w_b) = blocks
    cols, half = o_ref.shape[0], o_ref.shape[1] // 2
    rows = r_ref.shape[0]
    step = pl.program_id(0)

    def turned(ref, first, second):
        ref[0:cols, :] = first.T.astype(jnp.bfloat16)[0:cols]
        ref[cols : 2 * cols, :] = second.T.astype(jnp.bfloat16)[0:cols]

    @pl.when(step == 0)
    def _():
        rf = r_ref[...].astype(jnp.float32)
        zero = jnp.zeros_like(rf)
        e_ref[pl.ds(0, rows, stride=2), :] = rf
        e_ref[pl.ds(1, rows, stride=2), :] = zero
        f_ref[pl.ds(0, rows, stride=2), :] = zero
        f_ref[pl.ds(1, rows, stride=2), :] = rf
        turned(rt_ref, e_ref[...], f_ref[...])

    @pl.when(step == n_a)
    def _():
        for ref, (x, z) in zip(rb_refs, places(at_ref)):
            n = ref.shape[1]
            parts = []
            for src in (e_ref, f_ref):
                view = src.reshape(8, 2, 4, 24, LANES)
                parts.append(view[pl.ds(z, n // 48), :, pl.ds(x, 1)].reshape(n, LANES))
            turned(ref, *parts)

    def copies(at, first, g_ref, width):
        slot = lax.rem(at, 2)
        return [
            pltpu.make_async_copy(
                g_ref.at[slot, pl.ds(h * cols, cols), :],
                o_ref.at[:, pl.ds(pl.multiple_of(h * half + first + at * width, LANES), width)],
                sem.at[slot, h],
            )
            for h in range(2)
        ]

    def phase(here, count, first, g_ref, width, product):
        @pl.when((here >= 2) & (here < count))
        def _():
            for copy in copies(here - 2, first, g_ref, width):
                copy.wait()

        @pl.when((here >= 0) & (here < count))
        def _():
            g_ref[lax.rem(here, 2)] = product().astype(g_ref.dtype)
            for copy in copies(here, first, g_ref, width):
                copy.start()

        @pl.when(here == count - 1)
        def _():
            for back in range(min(2, count)):
                for copy in copies(here - back, first, g_ref, width):
                    copy.wait()

    def product_a():
        return jnp.dot(rt_ref[...], a_ref[...], preferred_element_type=jnp.float32)

    def product_b():
        total = None
        for ref, piece in zip(rb_refs, (own, near, far, half0, half1)):
            part = jnp.dot(ref[...], piece[...], preferred_element_type=jnp.float32)
            total = part if total is None else total + part
        return total

    phase(step, n_a, 0, ga_ref, w_a, product_a)
    phase(step - n_a, n_b, n_a * w_a, gb_ref, w_b, product_b)


def backward(at, returned, a, pieces, cols, n_a, n_b):
    rows, width_a = a.shape
    width_b = pieces[0].shape[1]
    w_a, w_b = width_a // n_a, width_b // n_b
    return pl.pallas_call(
        functools.partial(backward_kernel, ((n_a, w_a), (n_b, w_b))),
        grid=(n_a + n_b,),
        in_specs=[
            pl.BlockSpec(memory_space=pltpu.SMEM),
            pl.BlockSpec((rows // 2, LANES), lambda j: (0, 0)),
            pl.BlockSpec((rows, w_a), lambda j: (0, jnp.minimum(j, n_a - 1))),
        ]
        + [
            pl.BlockSpec((p.shape[0], w_b), lambda j: (0, jnp.maximum(j - n_a, 0))) for p in pieces
        ],
        out_specs=pl.BlockSpec(memory_space=pl.ANY),
        out_shape=jax.ShapeDtypeStruct((cols, 2 * (width_a + width_b)), jnp.bfloat16),
        scratch_shapes=[
            pltpu.VMEM((rows, LANES), jnp.float32),
            pltpu.VMEM((rows, LANES), jnp.float32),
            pltpu.VMEM((2 * cols, rows), jnp.bfloat16),
        ]
        + [pltpu.VMEM((2 * cols, p.shape[0]), jnp.bfloat16) for p in pieces]
        + [
            pltpu.VMEM((2, 2 * cols, w_a), jnp.bfloat16),
            pltpu.VMEM((2, 2 * cols, w_b), jnp.bfloat16),
            pltpu.SemaphoreType.DMA((2, 2)),
        ],
        cost_estimate=pl.CostEstimate(
            flops=2 * rows * (width_a + width_b) * 2 * cols,
            bytes_accessed=2 * rows * (width_a + width_b) + 4 * cols * (width_a + width_b),
            transcendentals=0,
        ),
    )(at, returned, a, *pieces)


def gathered(own, width_a):
    xs = lax.axis_size("x")
    core = lax.axis_index("c")
    own_a, own_b = own[:, :width_a], own[:, width_a:]
    b = lax.all_gather(own_b, ("z", "c"), axis=0, tiled=True)
    a = lax.all_gather(own_a, "x", axis=0, tiled=True)
    a = lax.all_gather(a, ("z", "c"), axis=0, tiled=True)

    onward = [
        (x * 2 + c, (x + 1 - 2 * c) % xs * 2 + c) for x in range(xs) for c in range(2)
    ]
    swap = [(0, 1), (1, 0)]
    near = lax.ppermute(b, ("x", "c"), onward)
    count = near.shape[0] // 2
    half = lax.dynamic_slice_in_dim(near, core * count, count, axis=0)
    half0 = lax.ppermute(half, ("x", "c"), onward)
    far = lax.ppermute(near, "c", swap)
    half1 = lax.ppermute(half0, "c", swap)
    return a, (b, near, far, half0, half1)


def local(expert_hidden, probe_tangent, routed_experts, gate_weights):
    tensor = ("z", "x", "c")
    experts = lax.axis_size("expert")
    parts = lax.axis_size(tensor)
    hidden = expert_hidden[0]
    probe = probe_tangent[0]
    cols = probe.shape[0]
    toks = routed_experts.shape[0]
    capacity = hidden.shape[0] * parts // experts

    own = hidden.reshape(2 * hidden.shape[0], hidden.shape[1] // 2)
    width_a = WIDTH_A
    a, pieces = gathered(own, width_a)
    at = jnp.stack([lax.axis_index("x"), lax.axis_index("c")]).astype(jnp.int32)

    ids = routed_experts.reshape(-1)
    one_hot = (ids[:, None] == jnp.arange(experts, dtype=jnp.int32)[None, :]).astype(jnp.int32)
    earlier = jnp.cumsum(one_hot, axis=0) - one_hot
    rank = jnp.sum(one_hot * earlier, axis=1)
    chip, core, place = rank // 24, rank % 24 // 12, rank % 12
    row = (ids * capacity + core * (capacity // 2) + chip * 12 + place).reshape(toks, 2)

    partial = forward_b(at, pieces, probe, width_a)
    tangent = forward_a(a, probe, partial.reshape(a.shape[0], 2 * LANES))
    tangent = lax.all_to_all(
        tangent.reshape(experts, capacity, LANES), "expert", split_axis=0, concat_axis=0, tiled=True
    )
    back, squares = combine(tangent.reshape(experts * capacity, LANES), row, gate_weights)
    back = lax.all_to_all(
        back.reshape(experts, capacity, LANES),
        "expert",
        split_axis=0,
        concat_axis=0,
        tiled=True,
    )
    shares = lax.all_gather(squares[0:1], ("x", "c"), axis=0, tiled=True)
    shares = jnp.sum(shares, axis=0)
    shares = jnp.broadcast_to(shares[None, None], (lax.axis_size("z"), 1, toks))
    shares = lax.all_to_all(shares, "z", split_axis=0, concat_axis=0, tiled=True)
    gradient = backward(
        at, back.reshape(experts * capacity, LANES), a, pieces, cols, BLOCKS_A, BLOCKS_B
    )
    quadratic = jnp.sum(shares, axis=(0, 1)) / (cols * parts)
    return gradient[None], quadratic


def solution(mesh):
    grid = Mesh(mesh.devices.reshape(8, 8, 4, 2), ("expert", "z", "x", "c"))
    tensor = ("z", "x", "c")
    return jax.shard_map(
        local,
        mesh=grid,
        in_specs=(
            P("expert", tensor, None),
            P("expert", tensor, None),
            P("expert", None),
            P("expert", None),
        ),
        out_specs=(P("expert", tensor, None), P("expert")),
        check_vma=False,
    )
```

time: 188 us -> 197 us (1.048)
  waiting for transfers between devices: 118 us -> 77.1 us
  starting transfers between devices: 9.89 us -> 26.3 us
  blocking collectives: 17.3 us -> 30.6 us
  local copies, waits for them, and re-layouts: 6.12 us -> 14.9 us
  Pallas kernels: 18.8 us -> 24.9 us
  other arithmetic: 3 us -> 7.54 us
    all_gather x1 -> x2, waiting for transfers between devices: 102 us -> 38.7 us  [the longest x1 38.7 us: gathered(): b = lax.all_gather(own_b, ('z', 'c'), axis=0, tiled=True)]
    ppermute x0 -> x4, waiting for transfers between devices: none -> 21.4 us  [the longest x1 19.8 us: gathered(): near = lax.ppermute(b, ('x', 'c'), onward)]
    all_gather x0 -> x2, blocking collectives: none -> 20.5 us  [the longest x1 11.4 us: gathered(): a = lax.all_gather(own_a, 'x', axis=0, tiled=True)]
    ppermute x0 -> x4, starting transfers between devices: none -> 16.3 us  [the longest x1 5.31 us: gathered(): half0 = lax.ppermute(half, ('x', 'c'), onward)]
    all_to_all x1, blocking collectives: 17.3 us -> 10 us  [local(): lax.all_to_all(shares, 'z', split_axis=0, concat_axis=0, tiled=True)]
    pallas_call x2 -> x3, Pallas kernels: 16.3 us -> 22.4 us  [the longest x1 9.52 us: backward(): pl.pallas_call(functools.partial(backward_kernel, ((n_a, w_a), (n_b, w_b)...]
    eq x2, local copies, waits for them, and re-layouts: 0.28 us -> 2.62 us  [local(): ids[:, None] == jnp.arange(experts, dtype=jnp.int32)[None, :]]
    all_to_all x1, waiting for transfers between devices: 6.79 us -> 9.05 us  [local(): lax.all_to_all(tangent.reshape(experts, capacity, LANES), 'expert', split...]
  transfers between devices with their start and end apart: 3 -> 8, of which waited for: 3 -> 5; matrix products, arithmetic and copies ran while one was open for 3% -> 9% of each run, Pallas kernels for 0% -> 4%
where the time goes in v2:
time: 197 us; the launch traced here: 195 us
  waiting for transfers between devices  77.1 us (39%)
  blocking collectives  30.6 us (16%)
  starting transfers between devices  26.3 us (13%)
  Pallas kernels  24.9 us (13%)
  local copies, waits for them, and re-layouts  14.9 us (8%)
  between operations  14.2 us (7%)
  other arithmetic  7.54 us (4%)
    all_gather x1, waiting for transfers between devices, gathered(): b = lax.all_gather(own_b, ('z', 'c'), axis=0, tiled=True)  38.7 us
    ppermute x1, waiting for transfers between devices, gathered(): near = lax.ppermute(b, ('x', 'c'), onward)  19.8 us
    all_gather x1, blocking collectives, gathered(): a = lax.all_gather(own_a, 'x', axis=0, tiled=True)  11.4 us
    all_to_all x1, blocking collectives, local(): lax.all_to_all(shares, 'z', split_axis=0, concat_axis=0, tiled=True)  10 us
    pallas_call x1, Pallas kernels, backward(): pl.pallas_call(functools.partial(backward_kernel, ((n_a, w_a), (n_b, w_b)...  9.52 us
    all_gather x1, blocking collectives, local(): shares = lax.all_gather(squares[0:1], ('x', 'c'), axis=0, tiled=True)  9.07 us
    all_to_all x1, waiting for transfers between devices, local(): lax.all_to_all(tangent.reshape(experts, capacity, LANES), 'expert', split...  9.05 us
    all_to_all x1, waiting for transfers between devices, local(): lax.all_to_all(back.reshape(experts, capacity, LANES), 'expert', split_ax...  7.89 us
  transfers between devices with their start and end apart: 8, of which 5 were waited for; matrix products, arithmetic and copies ran while one was open for 9% of the time, Pallas kernels for 4%

profile of v2, /device:TPU:1, one launch (start us, length us, event | category | flops | bytes accessed | tf_op | source)
XLA Modules:
  0.0 195.4 jit_solution(4943055556741669359)
XLA Ops:
  7.2 1.0 reshape_squeeze.3
  9.0 11.4 %all_gather.12 = bf16[96,1792]{1,0:T(8,128)(2,1)} all-gather(bf16[24,1792]{1,0:T(8,128)(2,1)S(1)} %slice.20), channel_id=1, replica_groups=mesh['expert'=8,'z'=8,'x'=4,'c'=2] {'x'}, dimensions={0}, use_global_device_ids=true | all-gather | bytes 430080 | tf_op jit(solution)/shard_map/all_gather | solution.py:251
  20.5 38.7 %all-gather.6.cloned.1.call-done.own = bf16[384,2304]{1,0:T(8,128)(2,1)} async-done(((bf16[24,2304]{1,0:T(8,128)(2,1)}), bf16[384,2304]{1,0:T(8,128)(2,1)}) %all-gather.6.cloned.1.call-update) | async-done | bytes 1769488 | tf_op jit(solution)/shard_map/all_gather | solution.py:250
  59.2 4.3 %collective-permute-start = (bf16[384,2304]{1,0:T(8,128)(2,1)}, bf16[384,2304]{1,0:T(8,128)(2,1)S(1)}, u32[]{:S(2)}, u32[]{:S(2)}) collective-permute-start(bf16[384,2304]{1,0:T(8,128)(2,1)} %all-gather.6.cloned.1.call-done.own), channel_id=1, source_target_pairs={{0,2},{1,7},{2,4},{3,1},{4,6},{5,3},{6,0},{7,5},{8,10},{9,15},{10,... | collective-permute-start | bytes 5308424 | tf_op jit(solution)/shard_map/ppermute | solution.py:258
  63.5 19.8 %collective-permute-done.near = bf16[384,2304]{1,0:T(8,128)(2,1)S(1)} collective-permute-done((bf16[384,2304]{1,0:T(8,128)(2,1)}, bf16[384,2304]{1,0:T(8,128)(2,1)S(1)}, u32[]{:S(2)}, u32[]{:S(2)}) %collective-permute-start) | collective-permute-done | bytes 1769504 | tf_op jit(solution)/shard_map/ppermute | solution.py:258
  83.3 1.0 constant_dynamic-slice_fusion
  84.3 5.3 %collective-permute-start.2 = (bf16[192,2304]{1,0:T(8,128)(2,1)}, bf16[192,2304]{1,0:T(8,128)(2,1)}, u32[]{:S(2)}, u32[]{:S(2)}) collective-permute-start(bf16[192,2304]{1,0:T(8,128)(2,1)} %constant_dynamic-slice_fusion), channel_id=1, source_target_pairs={{0,2},{1,7},{2,4},{3,1},{4,6},{5,3},{6,0},{7,5},{8,10},{9,15},{10,... | collective-permute-start | bytes 2654216 | tf_op jit(solution)/shard_map/ppermute | solution.py:261
  89.6 1.9 collective-permute-start.1
  91.6 0.8 copy.45
  92.4 1.0 eq.32
  93.4 1.6 eq.28
  95.6 1.9 reduce-window.6
  98.3 1.6 collective-permute-done.2.half0
  99.9 4.8 %collective-permute-start.3 = (bf16[192,2304]{1,0:T(8,128)(2,1)}, bf16[192,2304]{1,0:T(8,128)(2,1)}, u32[]{:S(2)}, u32[]{:S(2)}) collective-permute-start(bf16[192,2304]{1,0:T(8,128)(2,1)} %collective-permute-done.2.half0), channel_id=1, source_target_pairs={{0,1},{1,0},{2,3},{3,2},{4,5},{5,4},{6,7},{7,6},{8,9},{9,8},{10,11... | collective-permute-start | bytes 2654216 | tf_op jit(solution)/shard_map/ppermute | solution.py:263
  105.5 0.8 rem.38
  106.3 0.8 div.23
  107.1 0.8 ne.52
  107.8 1.7 add_select_fusion.2
  109.6 1.0 copy.48
  110.5 1.0 copy.47
  112.2 1.2 copy-done.1
  113.4 6.9 %shard_map.59 = f32[8,2,4,24,256]{4,3,2,1,0:T(8,128)} custom-call(s32[2]{0:T(128)} %pad_add_fusion.at_ref, bf16[384,2304]{1,0:T(8,128)(2,1)} %all-gather.6.cloned.1.call-done.own, bf16[384,2304]{1,0:T(8,128)(2,1)} %copy-done, bf16[384,2304]{1,0:T(8,128)(2,1)} %copy-done.1, bf16[192,2304]{1,0:T(8,128)(2,1)} %collective-permute-done.2.half0, ...), custom_call_target="tpu_custom_call" | custom-call | flops 1811939328 | bytes 8650752 | tf_op jit(solution)/shard_map/pallas_call | solution.py:47
  120.3 6.0 %shard_map.60 = bf16[768,128]{1,0:T(8,128)(2,1)} custom-call(bf16[1536,1792]{1,0:T(8,128)(2,1)} %all-gather.4.cloned.1.call-done.x_ref.a_ref, bf16[96,8192]{1,0:T(8,128)(2,1)} %bitcast.21, f32[1536,256]{1,0:T(8,128)} %bitcast.22), custom_call_target="tpu_custom_call" | custom-call | tf_op jit(solution)/shard_map/pallas_call | solution.py:77
  126.2 6.5 %all-to-all-start = ((bf16[8,96,128]{2,1,0:T(8,128)(2,1)}), bf16[8,96,128]{2,1,0:T(8,128)(2,1)S(1)}, u32[]{:S(2)}, u32[]{:S(2)}) async-start(bf16[8,96,128]{2,1,0:T(8,128)(2,1)} %bitcast.26), calls=%async_computation | async-start | bytes 393216 | tf_op jit(solution)/shard_map/all_to_all | solution.py:291
  133.0 0.8 copy.50.gate_ref
  134.4 9.1 %all-to-all-done = bf16[8,96,128]{2,1,0:T(8,128)(2,1)S(1)} async-done(((bf16[8,96,128]{2,1,0:T(8,128)(2,1)}), bf16[8,96,128]{2,1,0:T(8,128)(2,1)S(1)}, u32[]{:S(2)}, u32[]{:S(2)}) %all-to-all-start) | async-done | bytes 196640 | tf_op jit(solution)/shard_map/all_to_all | solution.py:291
  144.2 2.5 %shard_map.61 = (bf16[768,128]{1,0:T(8,128)(2,1)}, f32[8,192]{1,0:T(8,128)}) custom-call(bf16[768,128]{1,0:T(8,128)(2,1)} %bitcast.25, s32[192,2]{1,0:T(8,128)} %fusion.1.row_ref, f32[192,2]{1,0:T(8,128)} %copy.50.gate_ref), custom_call_target="tpu_custom_call" | custom-call | tf_op jit(solution)/shard_map/pallas_call | solution.py:124
  147.3 9.1 %all-gather = f32[8,1,192]{2,1,0:T(1,128)S(1)} all-gather(f32[1,1,192]{2,1,0:T(1,128)S(1)} %slice_bitcast_fusion), channel_id=1, replica_groups=mesh['expert'=8,'z'=8,'x'=4,'c'=2] {'x','c'}, dimensions={0}, use_global_device_ids=true | all-gather | bytes 6912 | tf_op jit(solution)/shard_map/all_gather | solution.py:302
  156.5 10.0 %all_to_all.15 = f32[8,1,192]{2,1,0:T(1,128)S(1)} all-to-all(f32[8,1,192]{2,1,0:T(1,128)S(1)} %broadcast_in_dim.5), channel_id=1, replica_groups=mesh['expert'=8,'z'=8,'x'=4,'c'=2] {'z'}, dimensions={0} | all-to-all | bytes 12288 | tf_op jit(solution)/shard_map/all_to_all | solution.py:305
  166.5 3.4 %all-to-all-start.1 = ((bf16[8,96,128]{2,1,0:T(8,128)(2,1)}), bf16[8,96,128]{2,1,0:T(8,128)(2,1)S(1)}, u32[]{:S(2)}, u32[]{:S(2)}) async-start(bf16[8,96,128]{2,1,0:T(8,128)(2,1)} %bitcast.27), calls=%async_computation.1 | async-start | bytes 393216 | tf_op jit(solution)/shard_map/all_to_all | solution.py:295
  170.5 7.9 %all-to-all-done.1 = bf16[8,96,128]{2,1,0:T(8,128)(2,1)S(1)} async-done(((bf16[8,96,128]{2,1,0:T(8,128)(2,1)}), bf16[8,96,128]{2,1,0:T(8,128)(2,1)S(1)}, u32[]{:S(2)}, u32[]{:S(2)}) %all-to-all-start.1) | async-done | bytes 196640 | tf_op jit(solution)/shard_map/all_to_all | solution.py:295
  179.1 9.5 %shard_map.62 = bf16[96,8192]{1,0:T(8,128)(2,1)} custom-call(s32[2]{0:T(128)} %pad_add_fusion.at_ref, bf16[768,128]{1,0:T(8,128)(2,1)} %bitcast.24, bf16[1536,1792]{1,0:T(8,128)(2,1)} %all-gather.4.cloned.1.call-done.x_ref.a_ref, bf16[384,2304]{1,0:T(8,128)(2,1)} %all-gather.6.cloned.1.call-done.own, bf16[384,2304]{1,0:T(8,128)(2,1)} %copy-done, ...), custom_call_target="tpu_custom_call" | custom-call | flops 2415919104 | bytes 14155776 | tf_op jit(solution)/shard_map/pallas_call | solution.py:214
  (38 shorter events, 7.2 us)
Async XLA Ops:
  7.2 84.4 %copy-start.4 = (s32[192,2]{0,1:T(2,128)S(1)}, s32[192,2]{0,1:T(2,128)}, u32[]{:S(2)}) copy-start(s32[192,2]{0,1:T(2,128)} %param.6) | copy-start | bytes 4612
  7.2 52.0 %all-gather.6.cloned.1.call-start = ((), (), s32[]{:S(2)}) async-start(), calls=%async_computation.4 | async-start | bytes 1880064 | tf_op jit(solution)/shard_map/all_gather | solution.py:250
  8.9 111.3 %all-gather.4.cloned.1.call-start = ((), (), s32[]{:S(2)}) async-start(), calls=%async_computation.3 | async-start | bytes 5849088 | tf_op jit(solution)/shard_map/all_gather | solution.py:252
  59.2 24.1 %collective-permute-start = (bf16[384,2304]{1,0:T(8,128)(2,1)}, bf16[384,2304]{1,0:T(8,128)(2,1)S(1)}, u32[]{:S(2)}, u32[]{:S(2)}) collective-permute-start(bf16[384,2304]{1,0:T(8,128)(2,1)} %all-gather.6.cloned.1.call-done.own), channel_id=1, source_target_pairs={{0,2},{1,7},{2,4},{3,1},{4,6},{5,3},{6,0},{7,5},{8,10},{9,15},{10,... | collective-permute-start | bytes 5308424 | tf_op jit(solution)/shard_map/ppermute | solution.py:258
  83.3 28.9 %copy-start = (bf16[384,2304]{1,0:T(8,128)(2,1)}, bf16[384,2304]{1,0:T(8,128)(2,1)S(1)}, u32[]{:S(2)}) copy-start(bf16[384,2304]{1,0:T(8,128)(2,1)S(1)} %collective-permute-done.near) | copy-start | bytes 5308420
  84.3 15.6 %collective-permute-start.2 = (bf16[192,2304]{1,0:T(8,128)(2,1)}, bf16[192,2304]{1,0:T(8,128)(2,1)}, u32[]{:S(2)}, u32[]{:S(2)}) collective-permute-start(bf16[192,2304]{1,0:T(8,128)(2,1)} %constant_dynamic-slice_fusion), channel_id=1, source_target_pairs={{0,2},{1,7},{2,4},{3,1},{4,6},{5,3},{6,0},{7,5},{8,10},{9,15},{10,... | collective-permute-start | bytes 2654216 | tf_op jit(solution)/shard_map/ppermute | solution.py:261
  89.6 22.5 %collective-permute-start.1 = (bf16[384,2304]{1,0:T(8,128)(2,1)S(1)}, bf16[384,2304]{1,0:T(8,128)(2,1)S(1)}, u32[]{:S(2)}, u32[]{:S(2)}) collective-permute-start(bf16[384,2304]{1,0:T(8,128)(2,1)S(1)} %collective-permute-done.near), channel_id=1, source_target_pairs={{0,1},{1,0},{2,3},{3,2},{4,5},{5,4},{6,7},{7,6},{8,9},{9,8},{10,11... | collective-permute-start | bytes 5308424 | tf_op jit(solution)/shard_map/ppermute | solution.py:262
  99.9 12.2 %collective-permute-start.3 = (bf16[192,2304]{1,0:T(8,128)(2,1)}, bf16[192,2304]{1,0:T(8,128)(2,1)}, u32[]{:S(2)}, u32[]{:S(2)}) collective-permute-start(bf16[192,2304]{1,0:T(8,128)(2,1)} %collective-permute-done.2.half0), channel_id=1, source_target_pairs={{0,1},{1,0},{2,3},{3,2},{4,5},{5,4},{6,7},{7,6},{8,9},{9,8},{10,11... | collective-permute-start | bytes 2654216 | tf_op jit(solution)/shard_map/ppermute | solution.py:263
  112.1 1.2 copy-start.1
  120.2 12.5 %copy-start.5 = (s32[192,2]{0,1:T(2,128)S(1)}, s32[192,2]{0,1:T(2,128)}, u32[]{:S(2)}) copy-start(s32[192,2]{0,1:T(2,128)} %param.6) | copy-start | bytes 4612
  120.2 12.8 %copy-start.6 = (f32[192,2]{0,1:T(2,128)S(1)}, f32[192,2]{0,1:T(2,128)}, u32[]{:S(2)}) copy-start(f32[192,2]{0,1:T(2,128)} %param.7) | copy-start | bytes 4612
  126.2 17.2 %all-to-all-start = ((bf16[8,96,128]{2,1,0:T(8,128)(2,1)}), bf16[8,96,128]{2,1,0:T(8,128)(2,1)S(1)}, u32[]{:S(2)}, u32[]{:S(2)}) async-start(bf16[8,96,128]{2,1,0:T(8,128)(2,1)} %bitcast.26), calls=%async_computation | async-start | bytes 393216 | tf_op jit(solution)/shard_map/all_to_all | solution.py:291
  143.5 0.7 copy-start.3
  166.5 11.9 %all-to-all-start.1 = ((bf16[8,96,128]{2,1,0:T(8,128)(2,1)}), bf16[8,96,128]{2,1,0:T(8,128)(2,1)S(1)}, u32[]{:S(2)}, u32[]{:S(2)}) async-start(bf16[8,96,128]{2,1,0:T(8,128)(2,1)} %bitcast.27), calls=%async_computation.1 | async-start | bytes 393216 | tf_op jit(solution)/shard_map/all_to_all | solution.py:295
  178.4 0.7 copy-start.2
Sparse Core Ops, SparseCore 0:
  10.7 48.4 all-gather.5
  61.3 45.3 all-gather.3

commit v3 on v2

v3 whole, which is shorter than its diff:
```python
import functools

import jax
import jax.numpy as jnp
from jax import lax
from jax.experimental import pallas as pl
from jax.experimental.pallas import tpu as pltpu
from jax.sharding import Mesh, PartitionSpec as P


LANES = 128
WIDTH_A, BLOCKS_A, BLOCKS_B = 2304, 2, 2


def stack_probe(pc_ref, p_ref, start):
    cols, half, width = p_ref.shape[0], p_ref.shape[1] // 2, pc_ref.shape[1]
    pc_ref[...] = jnp.zeros_like(pc_ref)
    pc_ref[0:cols, :] = p_ref[:, start : start + width]
    pc_ref[LANES : LANES + cols, :] = p_ref[:, half + start : half + start + width]


def times(x, y):
    return lax.dot_general(x, y, (((1,), (1,)), ((), ())), preferred_element_type=jnp.float32)


def piece_copies(pieces, all_ref, sem):
    x, core = lax.axis_index("x"), lax.axis_index("c")
    toward = 1 - 2 * core
    behind = lax.rem(x - toward + 4, 4)
    ahead = lax.rem(x + toward + 4, 4)
    across = lax.rem(x + 2, 4)
    other = 1 - core
    spots = (
        (core, x), (other, x), (core, behind), (other, behind),
        (other, ahead), (core, ahead), (core, across), (other, across),
    )
    return [
        pltpu.make_async_copy(piece, all_ref.at[:, c, at], sem.at[i])
        for i, (piece, (c, at)) in enumerate(zip(pieces, spots))
    ]


def forward_b_kernel(start, *refs):
    pieces, (p_ref, y_ref, pc_ref, all_ref, sem) = refs[:8], refs[8:]
    copies = piece_copies(pieces, all_ref, sem)
    for copy in copies:
        copy.start()
    stack_probe(pc_ref, p_ref, start)
    for copy in copies:
        copy.wait()
    width = pc_ref.shape[1]
    rows = 384
    for i in range(y_ref.shape[0] // rows):
        block = all_ref[2 * i : 2 * i + 2].reshape(rows, width)
        y_ref[i * rows : (i + 1) * rows] = times(block, pc_ref[...])


def forward_b(pieces, probe, start):
    width = pieces[0].shape[-1]
    rows = 1536
    return pl.pallas_call(
        functools.partial(forward_b_kernel, start),
        in_specs=[pl.BlockSpec(memory_space=pl.ANY)] * 8
        + [pl.BlockSpec(memory_space=pltpu.VMEM)],
        out_specs=pl.BlockSpec(memory_space=pltpu.VMEM),
        out_shape=jax.ShapeDtypeStruct((rows, 2 * LANES), jnp.float32),
        scratch_shapes=[
            pltpu.VMEM((2 * LANES, width), jnp.bfloat16),
            pltpu.VMEM((8, 2, 4, 24, width), jnp.bfloat16),
            pltpu.SemaphoreType.DMA((8,)),
        ],
        cost_estimate=pl.CostEstimate(
            flops=2 * rows * width * 2 * LANES,
            bytes_accessed=2 * rows * width + 4 * rows * 2 * LANES,
            transcendentals=0,
        ),
    )(*pieces, probe)


def forward_a_kernel(x_ref, p_ref, yb_ref, o_ref, pc_ref, y0_ref, y1_ref):
    rows = o_ref.shape[0]

    @pl.when(pl.program_id(0) == 0)
    def _():
        stack_probe(pc_ref, p_ref, 0)

    y = times(x_ref[...], pc_ref[...]) + yb_ref[...]
    y0_ref[...] = y[:, 0:LANES]
    y1_ref[...] = y[:, LANES : 2 * LANES]
    total = y0_ref[pl.ds(0, rows, stride=2), :] + y1_ref[pl.ds(1, rows, stride=2), :]
    o_ref[...] = total.astype(o_ref.dtype)


def forward_a(x, probe, partial, block=384):
    rows, width = x.shape
    return pl.pallas_call(
        forward_a_kernel,
        grid=(rows // block,),
        in_specs=[
            pl.BlockSpec((block, width), lambda i: (i, 0)),
            pl.BlockSpec(probe.shape, lambda i: (0, 0)),
            pl.BlockSpec((block, 2 * LANES), lambda i: (i, 0)),
        ],
        out_specs=pl.BlockSpec((block // 2, LANES), lambda i: (i, 0)),
        out_shape=jax.ShapeDtypeStruct((rows // 2, LANES), jnp.bfloat16),
        scratch_shapes=[
            pltpu.VMEM((2 * LANES, width), jnp.bfloat16),
            pltpu.VMEM((block, LANES), jnp.float32),
            pltpu.VMEM((block, LANES), jnp.float32),
        ],
    )(x, probe, partial)


def combine_kernel(capacity, t_ref, id_ref, gate_ref, b_ref, q_ref):
    rows = t_ref.shape[0]
    toks = id_ref.shape[1]
    experts = lax.broadcasted_iota(jnp.int32, (8, toks), 0)
    named = [(experts == id_ref[k : k + 1, :]).astype(jnp.float32) for k in range(2)]
    before = lax.broadcasted_iota(jnp.int32, (toks, toks), 0)
    before = before < lax.broadcasted_iota(jnp.int32, (toks, toks), 1)
    counts = jnp.dot(
        (named[0] + named[1]).astype(jnp.bfloat16),
        before.astype(jnp.float32).astype(jnp.bfloat16),
        preferred_element_type=jnp.float32,
    )
    place = lax.broadcasted_iota(jnp.int32, (rows, toks), 0)
    picks = []
    total = None
    for k in range(2):
        rank = jnp.sum(named[k] * counts, axis=0, keepdims=True).astype(jnp.int32)
        dozen = jnp.right_shift(rank * 5462, 16)
        slot = (dozen & 1) * (capacity // 2) + jnp.right_shift(dozen, 1) * 12 + rank - dozen * 12
        row = id_ref[k : k + 1, :] * capacity + slot
        pick = (place == row).astype(jnp.float32).astype(jnp.bfloat16)
        part = lax.dot_general(
            t_ref[...], pick, (((0,), (0,)), ((), ())), preferred_element_type=jnp.float32
        )
        part = part * gate_ref[k : k + 1, :]
        total = part if total is None else total + part
        picks.append(pick)
    back = None
    for k in range(2):
        weighted = (total * gate_ref[k : k + 1, :]).astype(jnp.bfloat16)
        placed = lax.dot_general(
            picks[k], weighted, (((1,), (1,)), ((), ())), preferred_element_type=jnp.float32
        )
        back = placed if back is None else back + placed
    b_ref[...] = back.astype(b_ref.dtype)
    q_ref[...] = jnp.sum(total * total, axis=0, keepdims=True)


def combine(tangent, ids, gates, capacity):
    rows = tangent.shape[0]
    toks = ids.shape[1]
    return pl.pallas_call(
        functools.partial(combine_kernel, capacity),
        out_shape=(
            jax.ShapeDtypeStruct((rows, LANES), jnp.bfloat16),
            jax.ShapeDtypeStruct((1, toks), jnp.float32),
        ),
    )(tangent, ids, gates)


def backward_kernel(blocks, r_ref, a_ref, *refs):
    pieces, (o_ref, e_ref, f_ref, rt_ref, all_ref, ga_ref, gb_ref, in_sem, sem) = refs[:8], refs[8:]
    (n_a, w_a), (n_b, w_b) = blocks
    cols, half = o_ref.shape[0], o_ref.shape[1] // 2
    rows = r_ref.shape[0]
    step = pl.program_id(0)
    arrivals = piece_copies(pieces, all_ref, in_sem)

    @pl.when(step == 0)
    def _():
        for copy in arrivals:
            copy.start()
        rf = r_ref[...].astype(jnp.float32)
        zero = jnp.zeros_like(rf)
        e_ref[pl.ds(0, rows, stride=2), :] = rf
        e_ref[pl.ds(1, rows, stride=2), :] = zero
        f_ref[pl.ds(0, rows, stride=2), :] = zero
        f_ref[pl.ds(1, rows, stride=2), :] = rf
        rt_ref[0:cols, :] = e_ref[...].T.astype(jnp.bfloat16)[0:cols]
        rt_ref[cols : 2 * cols, :] = f_ref[...].T.astype(jnp.bfloat16)[0:cols]

    @pl.when(step == n_a)
    def _():
        for copy in arrivals:
            copy.wait()

    def copies(at, first, g_ref, width):
        slot = at % 2 if isinstance(at, int) else lax.rem(at, 2)
        return [
            pltpu.make_async_copy(
                g_ref.at[slot, pl.ds(h * cols, cols), :],
                o_ref.at[:, pl.ds(pl.multiple_of(h * half + first + at * width, LANES), width)],
                sem.at[slot, h],
            )
            for h in range(2)
        ]

    def phase(here, count, first, g_ref, width, product):
        @pl.when((here >= 2) & (here < count))
        def _():
            for copy in copies(here - 2, first, g_ref, width):
                copy.wait()

        @pl.when((here >= 0) & (here < count))
        def _():
            g_ref[lax.rem(here, 2)] = product().astype(g_ref.dtype)
            for copy in copies(here, first, g_ref, width):
                copy.start()

        @pl.when(here == count - 1)
        def _():
            for back in range(min(2, count)):
                for copy in copies(here - back, first, g_ref, width):
                    copy.wait()

    def product_a():
        return jnp.dot(rt_ref[...], a_ref[...], preferred_element_type=jnp.float32)

    def product_b():
        at = pl.multiple_of((step - n_a) * w_b, LANES)
        block = all_ref[:, :, :, :, pl.ds(at, w_b)].reshape(2 * rows, w_b)
        return jnp.dot(rt_ref[...], block, preferred_element_type=jnp.float32)

    phase(step, n_a, 0, ga_ref, w_a, product_a)
    phase(step - n_a, n_b, n_a * w_a, gb_ref, w_b, product_b)


def backward(returned, a, pieces, cols, n_a, n_b):
    rows, width_a = a.shape
    width_b = pieces[0].shape[-1]
    w_a, w_b = width_a // n_a, width_b // n_b
    return pl.pallas_call(
        functools.partial(backward_kernel, ((n_a, w_a), (n_b, w_b))),
        grid=(n_a + n_b,),
        in_specs=[
            pl.BlockSpec((rows // 2, LANES), lambda j: (0, 0)),
            pl.BlockSpec((rows, w_a), lambda j: (0, jnp.minimum(j, n_a - 1))),
        ]
        + [pl.BlockSpec(memory_space=pl.ANY)] * 8,
        out_specs=pl.BlockSpec(memory_space=pl.ANY),
        out_shape=jax.ShapeDtypeStruct((cols, 2 * (width_a + width_b)), jnp.bfloat16),
        scratch_shapes=[
            pltpu.VMEM((rows, LANES), jnp.float32),
            pltpu.VMEM((rows, LANES), jnp.float32),
            pltpu.VMEM((2 * cols, rows), jnp.bfloat16),
            pltpu.VMEM((8, 2, 4, 24, width_b), jnp.bfloat16),
            pltpu.VMEM((2, 2 * cols, w_a), jnp.bfloat16),
            pltpu.VMEM((2, 2 * cols, w_b), jnp.bfloat16),
            pltpu.SemaphoreType.DMA((8,)),
            pltpu.SemaphoreType.DMA((2, 2)),
        ],
        cost_estimate=pl.CostEstimate(
            flops=2 * rows * (width_a + width_b) * 2 * cols,
            bytes_accessed=2 * rows * (width_a + width_b) + 4 * cols * (width_a + width_b),
            transcendentals=0,
        ),
    )(returned, a, *pieces)


def gathered(own, width_a):
    xs, zs = lax.axis_size("x"), lax.axis_size("z")
    a = lax.all_gather(own[:, :width_a], "x", axis=0, tiled=True)
    copies = jnp.broadcast_to(own[None, :, width_a:], (zs, own.shape[0], own.shape[1] - width_a))
    copies, a = lax.optimization_barrier((copies, a))
    a = lax.all_gather(a, ("z", "c"), axis=0, tiled=True)
    b = lax.all_to_all(copies, "z", split_axis=0, concat_axis=0, tiled=True)

    onward = [(x * 2 + c, (x + 1 - 2 * c) % xs * 2 + c) for x in range(xs) for c in range(2)]

    def send(v):
        return lax.ppermute(v, ("x", "c"), onward)

    def swap(v):
        return lax.ppermute(v, "c", [(0, 1), (1, 0)])

    near0 = send(b)
    mate = swap(b)
    near1 = send(mate)
    across = send(near0)
    far0, far1 = swap(near0), swap(near1)
    return a, (b, mate, near0, near1, far0, far1, across, swap(across))


def local(expert_hidden, probe_tangent, routed_experts, gate_weights):
    tensor = ("z", "x", "c")
    experts = lax.axis_size("expert")
    parts = lax.axis_size(tensor)
    hidden = expert_hidden[0]
    probe = probe_tangent[0]
    cols = probe.shape[0]
    toks = routed_experts.shape[0]
    capacity = hidden.shape[0] * parts // experts

    own = hidden.reshape(2 * hidden.shape[0], hidden.shape[1] // 2)
    width_a = WIDTH_A
    a, pieces = gathered(own, width_a)
    partial = forward_b(pieces, probe, width_a)
    tangent = forward_a(a, probe, partial)
    tangent = lax.all_to_all(
        tangent.reshape(experts, capacity, LANES), "expert", split_axis=0, concat_axis=0, tiled=True
    )
    back, squares = combine(
        tangent.reshape(experts * capacity, LANES), routed_experts.T, gate_weights.T, capacity
    )
    back = lax.all_to_all(
        back.reshape(experts, capacity, LANES),
        "expert",
        split_axis=0,
        concat_axis=0,
        tiled=True,
    )
    shares = lax.all_gather(squares, ("x", "c"), axis=0, tiled=True)
    shares = jnp.sum(shares, axis=0)
    shares = jnp.broadcast_to(shares[None, None], (lax.axis_size("z"), 1, toks))
    shares = lax.all_to_all(shares, "z", split_axis=0, concat_axis=0, tiled=True)
    gradient = backward(
        back.reshape(experts * capacity, LANES), a, pieces, cols, BLOCKS_A, BLOCKS_B
    )
    quadratic = jnp.sum(shares, axis=(0, 1)) / (cols * parts)
    return gradient[None], quadratic


def solution(mesh):
    grid = Mesh(mesh.devices.reshape(8, 8, 4, 2), ("expert", "z", "x", "c"))
    tensor = ("z", "x", "c")
    return jax.shard_map(
        local,
        mesh=grid,
        in_specs=(
            P("expert", tensor, None),
            P("expert", tensor, None),
            P("expert", None),
            P("expert", None),
        ),
        out_specs=(P("expert", tensor, None), P("expert")),
        check_vma=False,
    )
```

time: 197 us -> 177 us (0.90)
  waiting for transfers between devices: 77.1 us -> 9.88 us
  blocking collectives: 30.6 us -> 75.6 us
  starting transfers between devices: 26.3 us -> 48.3 us
  local copies, waits for them, and re-layouts: 14.9 us -> 2.66 us
  other arithmetic: 7.54 us -> 0.62 us
    all_to_all x0 -> x2, blocking collectives: none -> 45.1 us  [the longest x1 28.5 us: gathered(): b = lax.all_to_all(copies, 'z', split_axis=0, concat_axis=0, tiled=True)]
    all_gather x1 -> x0, waiting for transfers between devices: 38.7 us -> none  [gathered(): b = lax.all_gather(own_b, ('z', 'c'), axis=0, tiled=True)]
    ppermute x4 -> x7, starting transfers between devices: 16.3 us -> 44.9 us  [the longest x4 36.5 us: swap(): return lax.ppermute(v, 'c', [(0, 1), (1, 0)])]
    ppermute x4 -> x7, waiting for transfers between devices: 21.4 us -> 2.01 us  [the longest x4 1.72 us: swap(): return lax.ppermute(v, 'c', [(0, 1), (1, 0)])]
    all_to_all x1 -> x0, waiting for transfers between devices: 9.05 us -> none  [local(): lax.all_to_all(tangent.reshape(experts, capacity, LANES), 'expert', split...]
    all_to_all x1 -> x0, starting transfers between devices: 6.46 us -> none  [local(): lax.all_to_all(tangent.reshape(experts, capacity, LANES), 'expert', split...]
    unnamed x17 -> x18, local copies, waits for them, and re-layouts: 4.82 us -> 1.56 us
    another operation x3 -> x0, other arithmetic: 3.15 us -> none
  transfers between devices with their start and end apart: 8 -> 9, of which waited for: 5 -> 3; matrix products, arithmetic and copies ran while one was open for 9% -> 0% of each run, Pallas kernels for 4% -> 4%
where the time goes in v3:
time: 177 us; the launch traced here: 175 us
  blocking collectives  75.6 us (43%)
  starting transfers between devices  48.3 us (27%)
  Pallas kernels  23.5 us (13%)
  between operations  14.3 us (8%)
  waiting for transfers between devices  9.88 us (6%)
  local copies, waits for them, and re-layouts  2.66 us (2%)
    ppermute x4, starting transfers between devices, swap(): return lax.ppermute(v, 'c', [(0, 1), (1, 0)])  36.5 us
    all_to_all x1, blocking collectives, gathered(): b = lax.all_to_all(copies, 'z', split_axis=0, concat_axis=0, tiled=True)  28.5 us
    all_to_all x1, blocking collectives, local(): lax.all_to_all(tangent.reshape(experts, capacity, LANES), 'expert', split...  16.6 us
    all_gather x1, blocking collectives, gathered(): a = lax.all_gather(own[:, :width_a], 'x', axis=0, tiled=True)  11.6 us
    all_gather x1, blocking collectives, local(): shares = lax.all_gather(squares, ('x', 'c'), axis=0, tiled=True)  9.96 us
    all_to_all x1, blocking collectives, local(): lax.all_to_all(shares, 'z', split_axis=0, concat_axis=0, tiled=True)  8.94 us
    ppermute x3, starting transfers between devices, send(): return lax.ppermute(v, ('x', 'c'), onward)  8.41 us
    all_to_all x1, waiting for transfers between devices, local(): lax.all_to_all(back.reshape(experts, capacity, LANES), 'expert', split_ax...  7.83 us
  transfers between devices with their start and end apart: 9, of which 3 were waited for; matrix products, arithmetic and copies ran while one was open for 0% of the time, Pallas kernels for 4%

profile of v3, /device:TPU:1, one launch (start us, length us, event | category | flops | bytes accessed | tf_op | source)
XLA Modules:
  0.0 174.9 jit_solution(17562963368696290139)
XLA Ops:
  7.2 0.0 all-gather.3.cloned.1.call-start
  7.2 1.0 reshape_squeeze.3
  8.3 11.6 %all_gather.9 = bf16[96,2304]{1,0:T(8,128)(2,1)} all-gather(bf16[24,2304]{1,0:T(8,128)(2,1)S(1)} %slice.9), channel_id=1, replica_groups=mesh['expert'=8,'z'=8,'x'=4,'c'=2] {'x'}, dimensions={0}, use_global_device_ids=true | all-gather | bytes 552960 | tf_op jit(solution)/shard_map/all_gather | solution.py:265
  20.0 0.0 all-gather.3.cloned.1.call-update
  20.0 28.5 %all_to_all.20.refs_0_ = bf16[8,24,1792]{2,1,0:T(8,128)(2,1)S(1)} all-to-all(bf16[8,24,1792]{2,1,0:T(8,128)(2,1)S(1)} %broadcast_in_dim.6), channel_id=1, replica_groups=mesh['expert'=8,'z'=8,'x'=4,'c'=2] {'z'}, dimensions={0} | all-to-all | bytes 1376256 | tf_op jit(solution)/shard_map/all_to_all | solution.py:269
  48.4 1.9 %collective-permute-start.1 = (bf16[8,24,1792]{2,1,0:T(8,128)(2,1)S(1)}, bf16[8,24,1792]{2,1,0:T(8,128)(2,1)S(1)}, u32[]{:S(2)}, u32[]{:S(2)}) collective-permute-start(bf16[8,24,1792]{2,1,0:T(8,128)(2,1)S(1)} %all_to_all.20.refs_0_), channel_id=1, source_target_pairs={{0,2},{1,7},{2,4},{3,1},{4,6},{5,3},{6,0},{7,5},{8,10},{9,15},{10,... | collective-permute-start | bytes 2064392 | tf_op jit(solution)/shard_map/ppermute | solution.py:274
  50.4 9.9 %collective-permute-start = (bf16[8,24,1792]{2,1,0:T(8,128)(2,1)S(1)}, bf16[8,24,1792]{2,1,0:T(8,128)(2,1)S(1)}, u32[]{:S(2)}, u32[]{:S(2)}) collective-permute-start(bf16[8,24,1792]{2,1,0:T(8,128)(2,1)S(1)} %all_to_all.20.refs_0_), channel_id=1, source_target_pairs={{0,1},{1,0},{2,3},{3,2},{4,5},{5,4},{6,7},{7,6},{8,9},{9,8},{10,11... | collective-permute-start | bytes 2064392 | tf_op jit(solution)/shard_map/ppermute | solution.py:277
  60.2 0.3 collective-permute-done.1.refs_2_
  60.5 4.6 %collective-permute-start.5 = (bf16[8,24,1792]{2,1,0:T(8,128)(2,1)S(1)}, bf16[8,24,1792]{2,1,0:T(8,128)(2,1)S(1)}, u32[]{:S(2)}, u32[]{:S(2)}) collective-permute-start(bf16[8,24,1792]{2,1,0:T(8,128)(2,1)S(1)} %collective-permute-done.1.refs_2_), channel_id=1, source_target_pairs={{0,2},{1,7},{2,4},{3,1},{4,6},{5,3},{6,0},{7,5},{8,10},{9,15},{10,... | collective-permute-start | bytes 2064392 | tf_op jit(solution)/shard_map/ppermute | solution.py:274
  65.1 0.0 collective-permute-done.refs_1_
  65.1 1.9 %collective-permute-start.2 = (bf16[8,24,1792]{2,1,0:T(8,128)(2,1)S(1)}, bf16[8,24,1792]{2,1,0:T(8,128)(2,1)S(1)}, u32[]{:S(2)}, u32[]{:S(2)}) collective-permute-start(bf16[8,24,1792]{2,1,0:T(8,128)(2,1)S(1)} %collective-permute-done.refs_1_), channel_id=1, source_target_pairs={{0,2},{1,7},{2,4},{3,1},{4,6},{5,3},{6,0},{7,5},{8,10},{9,15},{10,... | collective-permute-start | bytes 2064392 | tf_op jit(solution)/shard_map/ppermute | solution.py:274
  67.1 9.1 %collective-permute-start.3 = (bf16[8,24,1792]{2,1,0:T(8,128)(2,1)S(1)}, bf16[8,24,1792]{2,1,0:T(8,128)(2,1)S(1)}, u32[]{:S(2)}, u32[]{:S(2)}) collective-permute-start(bf16[8,24,1792]{2,1,0:T(8,128)(2,1)S(1)} %collective-permute-done.1.refs_2_), channel_id=1, source_target_pairs={{0,1},{1,0},{2,3},{3,2},{4,5},{5,4},{6,7},{7,6},{8,9},{9,8},{10,11... | collective-permute-start | bytes 2064392 | tf_op jit(solution)/shard_map/ppermute | solution.py:277
  76.2 0.0 collective-permute-done.5.refs_6_
  76.2 10.1 %collective-permute-start.6 = (bf16[8,24,1792]{2,1,0:T(8,128)(2,1)S(1)}, bf16[8,24,1792]{2,1,0:T(8,128)(2,1)S(1)}, u32[]{:S(2)}, u32[]{:S(2)}) collective-permute-start(bf16[8,24,1792]{2,1,0:T(8,128)(2,1)S(1)} %collective-permute-done.5.refs_6_), channel_id=1, source_target_pairs={{0,1},{1,0},{2,3},{3,2},{4,5},{5,4},{6,7},{7,6},{8,9},{9,8},{10,11... | collective-permute-start | bytes 2064392 | tf_op jit(solution)/shard_map/ppermute | solution.py:277
  86.4 0.0 collective-permute-done.2.refs_3_
  86.4 7.3 %collective-permute-start.4 = (bf16[8,24,1792]{2,1,0:T(8,128)(2,1)S(1)}, bf16[8,24,1792]{2,1,0:T(8,128)(2,1)S(1)}, u32[]{:S(2)}, u32[]{:S(2)}) collective-permute-start(bf16[8,24,1792]{2,1,0:T(8,128)(2,1)S(1)} %collective-permute-done.2.refs_3_), channel_id=1, source_target_pairs={{0,1},{1,0},{2,3},{3,2},{4,5},{5,4},{6,7},{7,6},{8,9},{9,8},{10,11... | collective-permute-start | bytes 2064392 | tf_op jit(solution)/shard_map/ppermute | solution.py:277
  93.7 0.0 collective-permute-done.3.refs_4_
  93.8 0.0 collective-permute-done.6.refs_7_
  93.8 1.7 collective-permute-done.4.refs_5_
  95.5 0.9 copy-done.7
  96.4 6.8 %shard_map.59.yb_ref = f32[1536,256]{1,0:T(8,128)} custom-call(bf16[8,24,1792]{2,1,0:T(8,128)(2,1)} %copy-done, bf16[8,24,1792]{2,1,0:T(8,128)(2,1)} %copy-done.2, bf16[8,24,1792]{2,1,0:T(8,128)(2,1)} %copy-done.1, bf16[8,24,1792]{2,1,0:T(8,128)(2,1)} %copy-done.4, bf16[8,24,1792]{2,1,0:T(8,128)(2,1)} %copy-done.5, bf16[8,24,1792]{2,1,0:T(8,128)(2,1)} %copy-done.7, ...), custom_call_target="tpu_custom_call" | custom-call | flops 1409286144 | bytes 7077888 | tf_op jit(solution)/shard_map/pallas_call | solution.py:61
  103.2 0.0 all-gather.3.cloned.1.call-done.x_ref.a_ref
  103.2 6.6 %shard_map.60 = bf16[768,128]{1,0:T(8,128)(2,1)} custom-call(bf16[1536,2304]{1,0:T(8,128)(2,1)} %all-gather.3.cloned.1.call-done.x_ref.a_ref, bf16[96,8192]{1,0:T(8,128)(2,1)} %bitcast.10, f32[1536,256]{1,0:T(8,128)} %shard_map.59.yb_ref), custom_call_target="tpu_custom_call" | custom-call | tf_op jit(solution)/shard_map/pallas_call | solution.py:96
  109.8 16.6 %all_to_all.21 = bf16[8,96,128]{2,1,0:T(8,128)(2,1)} all-to-all(bf16[8,96,128]{2,1,0:T(8,128)(2,1)} %bitcast.14), channel_id=1, replica_groups=mesh['expert'=8,'z'=8,'x'=4,'c'=2] {'expert'}, dimensions={0} | all-to-all | bytes 393216 | tf_op jit(solution)/shard_map/all_to_all | solution.py:302
  126.4 2.5 %shard_map.61 = (bf16[768,128]{1,0:T(8,128)(2,1)}, f32[1,192]{1,0:T(1,128)}) custom-call(bf16[768,128]{1,0:T(8,128)(2,1)} %bitcast.13, s32[2,192]{1,0:T(2,128)} %bitcast.16, f32[2,192]{1,0:T(2,128)} %bitcast.17), custom_call_target="tpu_custom_call" | custom-call | tf_op jit(solution)/shard_map/pallas_call | solution.py:155
  128.9 10.0 %all-gather = f32[8,1,192]{2,1,0:T(1,128)S(1)} all-gather(f32[1,1,192]{2,1,0:T(1,128)} %bitcast.18), channel_id=1, replica_groups=mesh['expert'=8,'z'=8,'x'=4,'c'=2] {'x','c'}, dimensions={0}, use_global_device_ids=true | all-gather | bytes 6912 | tf_op jit(solution)/shard_map/all_gather | solution.py:315
  138.9 8.9 %all_to_all.22 = f32[8,1,192]{2,1,0:T(1,128)S(1)} all-to-all(f32[8,1,192]{2,1,0:T(1,128)S(1)} %broadcast_in_dim.8), channel_id=1, replica_groups=mesh['expert'=8,'z'=8,'x'=4,'c'=2] {'z'}, dimensions={0} | all-to-all | bytes 12288 | tf_op jit(solution)/shard_map/all_to_all | solution.py:318
  147.9 3.4 %all-to-all-start.2 = ((bf16[8,96,128]{2,1,0:T(8,128)(2,1)}), bf16[8,96,128]{2,1,0:T(8,128)(2,1)S(1)}, u32[]{:S(2)}, u32[]{:S(2)}) async-start(bf16[8,96,128]{2,1,0:T(8,128)(2,1)} %bitcast.15), calls=%async_computation.2 | async-start | bytes 393216 | tf_op jit(solution)/shard_map/all_to_all | solution.py:308
  151.3 0.6 broadcast_multiply_fusion
  151.9 7.8 %all-to-all-done.2 = bf16[8,96,128]{2,1,0:T(8,128)(2,1)S(1)} async-done(((bf16[8,96,128]{2,1,0:T(8,128)(2,1)}), bf16[8,96,128]{2,1,0:T(8,128)(2,1)S(1)}, u32[]{:S(2)}, u32[]{:S(2)}) %all-to-all-start.2) | async-done | bytes 196640 | tf_op jit(solution)/shard_map/all_to_all | solution.py:308
  159.7 0.7 copy-done.8
  160.4 7.6 %shard_map.62 = bf16[96,8192]{1,0:T(8,128)(2,1)} custom-call(bf16[768,128]{1,0:T(8,128)(2,1)} %bitcast.12, bf16[1536,2304]{1,0:T(8,128)(2,1)} %all-gather.3.cloned.1.call-done.x_ref.a_ref, bf16[8,24,1792]{2,1,0:T(8,128)(2,1)} %copy-done, bf16[8,24,1792]{2,1,0:T(8,128)(2,1)} %copy-done.2, bf16[8,24,1792]{2,1,0:T(8,128)(2,1)} %copy-done.1, ...), custom_call_target="tpu_custom_call" | custom-call | flops 2415919104 | bytes 14155776 | tf_op jit(solution)/shard_map/pallas_call | solution.py:235
  (22 shorter events, 0.2 us)
Async XLA Ops:
  7.2 96.0 %all-gather.3.cloned.1.call-start = ((), (), s32[]{:S(2)}) async-start(), calls=%async_computation.4 | async-start | bytes 7520256 | tf_op jit(solution)/shard_map/all_gather | solution.py:268
  48.4 47.9 %copy-start = (bf16[8,24,1792]{2,1,0:T(8,128)(2,1)}, bf16[8,24,1792]{2,1,0:T(8,128)(2,1)S(1)}, u32[]{:S(2)}) copy-start(bf16[8,24,1792]{2,1,0:T(8,128)(2,1)S(1)} %all_to_all.20.refs_0_) | copy-start | bytes 2064388
  48.4 12.1 %collective-permute-start.1 = (bf16[8,24,1792]{2,1,0:T(8,128)(2,1)S(1)}, bf16[8,24,1792]{2,1,0:T(8,128)(2,1)S(1)}, u32[]{:S(2)}, u32[]{:S(2)}) collective-permute-start(bf16[8,24,1792]{2,1,0:T(8,128)(2,1)S(1)} %all_to_all.20.refs_0_), channel_id=1, source_target_pairs={{0,2},{1,7},{2,4},{3,1},{4,6},{5,3},{6,0},{7,5},{8,10},{9,15},{10,... | collective-permute-start | bytes 2064392 | tf_op jit(solution)/shard_map/ppermute | solution.py:274
  50.4 14.7 %collective-permute-start = (bf16[8,24,1792]{2,1,0:T(8,128)(2,1)S(1)}, bf16[8,24,1792]{2,1,0:T(8,128)(2,1)S(1)}, u32[]{:S(2)}, u32[]{:S(2)}) collective-permute-start(bf16[8,24,1792]{2,1,0:T(8,128)(2,1)S(1)} %all_to_all.20.refs_0_), channel_id=1, source_target_pairs={{0,1},{1,0},{2,3},{3,2},{4,5},{5,4},{6,7},{7,6},{8,9},{9,8},{10,11... | collective-permute-start | bytes 2064392 | tf_op jit(solution)/shard_map/ppermute | solution.py:277
  60.5 35.8 %copy-start.1 = (bf16[8,24,1792]{2,1,0:T(8,128)(2,1)}, bf16[8,24,1792]{2,1,0:T(8,128)(2,1)S(1)}, u32[]{:S(2)}) copy-start(bf16[8,24,1792]{2,1,0:T(8,128)(2,1)S(1)} %collective-permute-done.1.refs_2_) | copy-start | bytes 2064388
  60.5 15.7 %collective-permute-start.5 = (bf16[8,24,1792]{2,1,0:T(8,128)(2,1)S(1)}, bf16[8,24,1792]{2,1,0:T(8,128)(2,1)S(1)}, u32[]{:S(2)}, u32[]{:S(2)}) collective-permute-start(bf16[8,24,1792]{2,1,0:T(8,128)(2,1)S(1)} %collective-permute-done.1.refs_2_), channel_id=1, source_target_pairs={{0,2},{1,7},{2,4},{3,1},{4,6},{5,3},{6,0},{7,5},{8,10},{9,15},{10,... | collective-permute-start | bytes 2064392 | tf_op jit(solution)/shard_map/ppermute | solution.py:274
  65.1 31.2 %copy-start.2 = (bf16[8,24,1792]{2,1,0:T(8,128)(2,1)}, bf16[8,24,1792]{2,1,0:T(8,128)(2,1)S(1)}, u32[]{:S(2)}) copy-start(bf16[8,24,1792]{2,1,0:T(8,128)(2,1)S(1)} %collective-permute-done.refs_1_) | copy-start | bytes 2064388
  65.1 21.2 %collective-permute-start.2 = (bf16[8,24,1792]{2,1,0:T(8,128)(2,1)S(1)}, bf16[8,24,1792]{2,1,0:T(8,128)(2,1)S(1)}, u32[]{:S(2)}, u32[]{:S(2)}) collective-permute-start(bf16[8,24,1792]{2,1,0:T(8,128)(2,1)S(1)} %collective-permute-done.refs_1_), channel_id=1, source_target_pairs={{0,2},{1,7},{2,4},{3,1},{4,6},{5,3},{6,0},{7,5},{8,10},{9,15},{10,... | collective-permute-start | bytes 2064392 | tf_op jit(solution)/shard_map/ppermute | solution.py:274
  67.1 26.7 %collective-permute-start.3 = (bf16[8,24,1792]{2,1,0:T(8,128)(2,1)S(1)}, bf16[8,24,1792]{2,1,0:T(8,128)(2,1)S(1)}, u32[]{:S(2)}, u32[]{:S(2)}) collective-permute-start(bf16[8,24,1792]{2,1,0:T(8,128)(2,1)S(1)} %collective-permute-done.1.refs_2_), channel_id=1, source_target_pairs={{0,1},{1,0},{2,3},{3,2},{4,5},{5,4},{6,7},{7,6},{8,9},{9,8},{10,11... | collective-permute-start | bytes 2064392 | tf_op jit(solution)/shard_map/ppermute | solution.py:277
  76.2 20.1 %copy-start.3 = (bf16[8,24,1792]{2,1,0:T(8,128)(2,1)}, bf16[8,24,1792]{2,1,0:T(8,128)(2,1)S(1)}, u32[]{:S(2)}) copy-start(bf16[8,24,1792]{2,1,0:T(8,128)(2,1)S(1)} %collective-permute-done.5.refs_6_) | copy-start | bytes 2064388
  76.2 17.5 %collective-permute-start.6 = (bf16[8,24,1792]{2,1,0:T(8,128)(2,1)S(1)}, bf16[8,24,1792]{2,1,0:T(8,128)(2,1)S(1)}, u32[]{:S(2)}, u32[]{:S(2)}) collective-permute-start(bf16[8,24,1792]{2,1,0:T(8,128)(2,1)S(1)} %collective-permute-done.5.refs_6_), channel_id=1, source_target_pairs={{0,1},{1,0},{2,3},{3,2},{4,5},{5,4},{6,7},{7,6},{8,9},{9,8},{10,11... | collective-permute-start | bytes 2064392 | tf_op jit(solution)/shard_map/ppermute | solution.py:277
  86.4 10.0 %copy-start.4 = (bf16[8,24,1792]{2,1,0:T(8,128)(2,1)}, bf16[8,24,1792]{2,1,0:T(8,128)(2,1)S(1)}, u32[]{:S(2)}) copy-start(bf16[8,24,1792]{2,1,0:T(8,128)(2,1)S(1)} %collective-permute-done.2.refs_3_) | copy-start | bytes 2064388
  86.4 9.1 %collective-permute-start.4 = (bf16[8,24,1792]{2,1,0:T(8,128)(2,1)S(1)}, bf16[8,24,1792]{2,1,0:T(8,128)(2,1)S(1)}, u32[]{:S(2)}, u32[]{:S(2)}) collective-permute-start(bf16[8,24,1792]{2,1,0:T(8,128)(2,1)S(1)} %collective-permute-done.2.refs_3_), channel_id=1, source_target_pairs={{0,1},{1,0},{2,3},{3,2},{4,5},{5,4},{6,7},{7,6},{8,9},{9,8},{10,11... | collective-permute-start | bytes 2064392 | tf_op jit(solution)/shard_map/ppermute | solution.py:277
  93.7 1.7 copy-start.5
  93.8 1.7 copy-start.6
  95.5 0.9 copy-start.7
  147.9 11.8 %all-to-all-start.2 = ((bf16[8,96,128]{2,1,0:T(8,128)(2,1)}), bf16[8,96,128]{2,1,0:T(8,128)(2,1)S(1)}, u32[]{:S(2)}, u32[]{:S(2)}) async-start(bf16[8,96,128]{2,1,0:T(8,128)(2,1)} %bitcast.15), calls=%async_computation.2 | async-start | bytes 393216 | tf_op jit(solution)/shard_map/all_to_all | solution.py:308
  159.7 0.7 copy-start.8
Sparse Core Ops, SparseCore 0:
  20.1 64.3 all-gather.2

commit v4 on v3

--- a/solution.py
+++ b/solution.py
@@ -10,6 +10,7 @@
 
 LANES = 128
 WIDTH_A, BLOCKS_A, BLOCKS_B = 2304, 2, 2
+PIECES = 10
 
 
 def stack_probe(pc_ref, p_ref, start):
@@ -25,23 +26,21 @@
 
 def piece_copies(pieces, all_ref, sem):
     x, core = lax.axis_index("x"), lax.axis_index("c")
-    toward = 1 - 2 * core
-    behind = lax.rem(x - toward + 4, 4)
-    ahead = lax.rem(x + toward + 4, 4)
-    across = lax.rem(x + 2, 4)
     other = 1 - core
+    before, after, across = (x + 3) & 3, (x + 1) & 3, (x + 2) & 3
     spots = (
-        (core, x), (other, x), (core, behind), (other, behind),
-        (other, ahead), (core, ahead), (core, across), (other, across),
+        (0, core, x), (0, other, x),
+        (0, core, before), (0, core, after), (0, core, across), (4, core, across),
+        (0, other, before), (0, other, after), (0, other, across), (4, other, across),
     )
     return [
-        pltpu.make_async_copy(piece, all_ref.at[:, c, at], sem.at[i])
-        for i, (piece, (c, at)) in enumerate(zip(pieces, spots))
+        pltpu.make_async_copy(piece, all_ref.at[z : z + piece.shape[0], c, at], sem.at[i])
+        for i, (piece, (z, c, at)) in enumerate(zip(pieces, spots))
     ]
 
 
 def forward_b_kernel(start, *refs):
-    pieces, (p_ref, y_ref, pc_ref, all_ref, sem) = refs[:8], refs[8:]
+    pieces, (p_ref, y_ref, pc_ref, all_ref, sem) = refs[:PIECES], refs[PIECES:]
     copies = piece_copies(pieces, all_ref, sem)
     for copy in copies:
         copy.start()
@@ -60,14 +59,14 @@
     rows = 1536
     return pl.pallas_call(
         functools.partial(forward_b_kernel, start),
-        in_specs=[pl.BlockSpec(memory_space=pl.ANY)] * 8
+        in_specs=[pl.BlockSpec(memory_space=pl.ANY)] * PIECES
         + [pl.BlockSpec(memory_space=pltpu.VMEM)],
         out_specs=pl.BlockSpec(memory_space=pltpu.VMEM),
         out_shape=jax.ShapeDtypeStruct((rows, 2 * LANES), jnp.float32),
         scratch_shapes=[
             pltpu.VMEM((2 * LANES, width), jnp.bfloat16),
             pltpu.VMEM((8, 2, 4, 24, width), jnp.bfloat16),
-            pltpu.SemaphoreType.DMA((8,)),
+            pltpu.SemaphoreType.DMA((PIECES,)),
         ],
         cost_estimate=pl.CostEstimate(
             flops=2 * rows * width * 2 * LANES,
@@ -162,7 +161,7 @@
 
 
 def backward_kernel(blocks, r_ref, a_ref, *refs):
-    pieces, (o_ref, e_ref, f_ref, rt_ref, all_ref, ga_ref, gb_ref, in_sem, sem) = refs[:8], refs[8:]
+    pieces, (o_ref, e_ref, f_ref, rt_ref, all_ref, ga_ref, gb_ref, in_sem, sem) = refs[:PIECES], refs[PIECES:]
     (n_a, w_a), (n_b, w_b) = blocks
     cols, half = o_ref.shape[0], o_ref.shape[1] // 2
     rows = r_ref.shape[0]
@@ -239,7 +238,7 @@
             pl.BlockSpec((rows // 2, LANES), lambda j: (0, 0)),
             pl.BlockSpec((rows, w_a), lambda j: (0, jnp.minimum(j, n_a - 1))),
         ]
-        + [pl.BlockSpec(memory_space=pl.ANY)] * 8,
+        + [pl.BlockSpec(memory_space=pl.ANY)] * PIECES,
         out_specs=pl.BlockSpec(memory_space=pl.ANY),
         out_shape=jax.ShapeDtypeStruct((cols, 2 * (width_a + width_b)), jnp.bfloat16),
         scratch_shapes=[
@@ -249,7 +248,7 @@
             pltpu.VMEM((8, 2, 4, 24, width_b), jnp.bfloat16),
             pltpu.VMEM((2, 2 * cols, w_a), jnp.bfloat16),
             pltpu.VMEM((2, 2 * cols, w_b), jnp.bfloat16),
-            pltpu.SemaphoreType.DMA((8,)),
+            pltpu.SemaphoreType.DMA((PIECES,)),
             pltpu.SemaphoreType.DMA((2, 2)),
         ],
         cost_estimate=pl.CostEstimate(
@@ -261,27 +260,25 @@
 
 
 def gathered(own, width_a):
-    xs, zs = lax.axis_size("x"), lax.axis_size("z")
-    a = lax.all_gather(own[:, :width_a], "x", axis=0, tiled=True)
-    copies = jnp.broadcast_to(own[None, :, width_a:], (zs, own.shape[0], own.shape[1] - width_a))
-    copies, a = lax.optimization_barrier((copies, a))
+    xs = lax.axis_size("x")
+    a, own_b = own[:, :width_a], own[:, width_a:]
+    b = jnp.broadcast_to(own_b[None], (lax.axis_size("z"),) + own_b.shape)
+    b = lax.all_to_all(b, "z", split_axis=0, concat_axis=0, tiled=True)
+    a = lax.all_gather(a, "x", axis=0, tiled=True)
     a = lax.all_gather(a, ("z", "c"), axis=0, tiled=True)
-    b = lax.all_to_all(copies, "z", split_axis=0, concat_axis=0, tiled=True)
-
-    onward = [(x * 2 + c, (x + 1 - 2 * c) % xs * 2 + c) for x in range(xs) for c in range(2)]
-
-    def send(v):
-        return lax.ppermute(v, ("x", "c"), onward)
+
+    def send(v, step):
+        return lax.ppermute(v, "x", [(i, (i + step) % xs) for i in range(xs)])
 
     def swap(v):
         return lax.ppermute(v, "c", [(0, 1), (1, 0)])
 
-    near0 = send(b)
+    half = b.shape[0] // 2
+    fore, back = send(b, 1), send(b, -1)
     mate = swap(b)
-    near1 = send(mate)
-    across = send(near0)
-    far0, far1 = swap(near0), swap(near1)
-    return a, (b, mate, near0, near1, far0, far1, across, swap(across))
+    on0, on1 = send(fore[:half], 1), send(back[half:], -1)
+    mates = [swap(v) for v in (fore, back, on0, on1)]
+    return a, (b, mate, fore, back, on0, on1, *mates)
 
 
 def local(expert_hidden, probe_tangent, routed_experts, gate_weights):
@@ -312,10 +309,10 @@
         concat_axis=0,
         tiled=True,
     )
-    shares = lax.all_gather(squares, ("x", "c"), axis=0, tiled=True)
+    shares = lax.all_gather(squares, "x", axis=0, tiled=True)
     shares = jnp.sum(shares, axis=0)
-    shares = jnp.broadcast_to(shares[None, None], (lax.axis_size("z"), 1, toks))
-    shares = lax.all_to_all(shares, "z", split_axis=0, concat_axis=0, tiled=True)
+    shares = jnp.broadcast_to(shares[None, None], (lax.axis_size(("z", "c")), 1, toks))
+    shares = lax.all_to_all(shares, ("z", "c"), split_axis=0, concat_axis=0, tiled=True)
     gradient = backward(
         back.reshape(experts * capacity, LANES), a, pieces, cols, BLOCKS_A, BLOCKS_B
     )

time: 177 us -> 171 us (0.966)
  starting transfers between devices: 48.3 us -> 39.7 us
  blocking collectives: 75.6 us -> 77.9 us
    ppermute x4 -> x5, starting transfers between devices: 36.5 us -> 25.7 us  [swap(): return lax.ppermute(v, 'c', [(0, 1), (1, 0)])]
    all_to_all x2, blocking collectives: 37.4 us -> 42.5 us  [the longest x1 28.6 us: gathered(): b = lax.all_to_all(b, 'z', split_axis=0, concat_axis=0, tiled=True)]
    all_gather x2, blocking collectives: 21.6 us -> 18.9 us  [the longest x1 11.6 us: gathered(): a = lax.all_gather(a, 'x', axis=0, tiled=True)]
    ppermute x3 -> x4, starting transfers between devices: 8.41 us -> 10.6 us  [send(): return lax.ppermute(v, 'x', [(i, (i + step) % xs) for i in range(xs)])]
  transfers between devices with their start and end apart: 9 -> 11, of which waited for: 3 -> 2; matrix products, arithmetic and copies ran while one was open for 0% -> 0% of each run, Pallas kernels for 4% -> 4%
where the time goes in v4:
time: 171 us; the launch traced here: 170 us
  blocking collectives  77.9 us (46%)
  starting transfers between devices  39.7 us (23%)
  Pallas kernels  23.5 us (14%)
  between operations  14.3 us (8%)
  waiting for transfers between devices  10.5 us (6%)
  local copies, waits for them, and re-layouts  3.44 us (2%)
    all_to_all x1, blocking collectives, gathered(): b = lax.all_to_all(b, 'z', split_axis=0, concat_axis=0, tiled=True)  28.6 us
    ppermute x5, starting transfers between devices, swap(): return lax.ppermute(v, 'c', [(0, 1), (1, 0)])  25.7 us
    all_to_all x1, blocking collectives, local(): lax.all_to_all(tangent.reshape(experts, capacity, LANES), 'expert', split...  16.5 us
    all_to_all x1, blocking collectives, local(): lax.all_to_all(shares, ('z', 'c'), split_axis=0, concat_axis=0, tiled=True)  13.9 us
    all_gather x1, blocking collectives, gathered(): a = lax.all_gather(a, 'x', axis=0, tiled=True)  11.6 us
    ppermute x4, starting transfers between devices, send(): return lax.ppermute(v, 'x', [(i, (i + step) % xs) for i in range(xs)])  10.6 us
    all_to_all x1, waiting for transfers between devices, local(): lax.all_to_all(back.reshape(experts, capacity, LANES), 'expert', split_ax...  9.25 us
    pallas_call x1, Pallas kernels, backward(): pl.pallas_call(functools.partial(backward_kernel, ((n_a, w_a), (n_b, w_b)...  7.66 us
  transfers between devices with their start and end apart: 11, of which 2 were waited for; matrix products, arithmetic and copies ran while one was open for 0% of the time, Pallas kernels for 4%

profile of v4, /device:TPU:1, one launch (start us, length us, event | category | flops | bytes accessed | tf_op | source)
XLA Modules:
  0.0 170.0 jit_solution(343871283332568214)
XLA Ops:
  7.2 0.0 all-gather.3.cloned.1.call-start
  7.2 1.0 reshape_squeeze.3
  8.3 11.6 %all_gather.9 = bf16[96,2304]{1,0:T(8,128)(2,1)} all-gather(bf16[24,2304]{1,0:T(8,128)(2,1)S(1)} %slice.16), channel_id=1, replica_groups=mesh['expert'=8,'z'=8,'x'=4,'c'=2] {'x'}, dimensions={0}, use_global_device_ids=true | all-gather | bytes 552960 | tf_op jit(solution)/shard_map/all_gather | solution.py:267
  19.9 0.0 all-gather.3.cloned.1.call-update
  20.0 28.6 %all_to_all.20.refs_0_ = bf16[8,24,1792]{2,1,0:T(8,128)(2,1)S(1)} all-to-all(bf16[8,24,1792]{2,1,0:T(8,128)(2,1)S(1)} %broadcast_in_dim.6), channel_id=1, replica_groups=mesh['expert'=8,'z'=8,'x'=4,'c'=2] {'z'}, dimensions={0} | all-to-all | bytes 1376256 | tf_op jit(solution)/shard_map/all_to_all | solution.py:266
  48.6 1.9 %collective-permute-start.2 = (bf16[8,24,1792]{2,1,0:T(8,128)(2,1)S(1)}, bf16[8,24,1792]{2,1,0:T(8,128)(2,1)S(1)}, u32[]{:S(2)}, u32[]{:S(2)}) collective-permute-start(bf16[8,24,1792]{2,1,0:T(8,128)(2,1)S(1)} %all_to_all.20.refs_0_), channel_id=1, source_target_pairs={{0,6},{2,0},{4,2},{6,4},{1,7},{3,1},{5,3},{7,5},{8,14},{10,8},{12,... | collective-permute-start | bytes 2064392 | tf_op jit(solution)/shard_map/ppermute | solution.py:271
  50.5 3.4 %collective-permute-start.1 = (bf16[8,24,1792]{2,1,0:T(8,128)(2,1)S(1)}, bf16[8,24,1792]{2,1,0:T(8,128)(2,1)S(1)}, u32[]{:S(2)}, u32[]{:S(2)}) collective-permute-start(bf16[8,24,1792]{2,1,0:T(8,128)(2,1)S(1)} %all_to_all.20.refs_0_), channel_id=1, source_target_pairs={{0,2},{2,4},{4,6},{6,0},{1,3},{3,5},{5,7},{7,1},{8,10},{10,12},{12... | collective-permute-start | bytes 2064392 | tf_op jit(solution)/shard_map/ppermute | solution.py:271
  53.9 10.3 %collective-permute-start = (bf16[8,24,1792]{2,1,0:T(8,128)(2,1)S(1)}, bf16[8,24,1792]{2,1,0:T(8,128)(2,1)S(1)}, u32[]{:S(2)}, u32[]{:S(2)}) collective-permute-start(bf16[8,24,1792]{2,1,0:T(8,128)(2,1)S(1)} %all_to_all.20.refs_0_), channel_id=1, source_target_pairs={{0,1},{1,0},{2,3},{3,2},{4,5},{5,4},{6,7},{7,6},{8,9},{9,8},{10,11... | collective-permute-start | bytes 2064392 | tf_op jit(solution)/shard_map/ppermute | solution.py:274
  64.2 0.0 collective-permute-done.2.refs_3_
  64.3 3.2 %collective-permute-start.4 = (bf16[4,24,1792]{2,1,0:T(8,128)(2,1)S(1)}, bf16[4,24,1792]{2,1,0:T(8,128)(2,1)S(1)}, u32[]{:S(2)}, u32[]{:S(2)}) collective-permute-start(bf16[4,24,1792]{2,1,0:T(8,128)(2,1)S(1)} %slice.19), channel_id=1, source_target_pairs={{0,6},{2,0},{4,2},{6,4},{1,7},{3,1},{5,3},{7,5},{8,14},{10,8},{12,... | collective-permute-start | bytes 1032200 | tf_op jit(solution)/shard_map/ppermute | solution.py:271
  67.5 2.1 %collective-permute-start.3 = (bf16[4,24,1792]{2,1,0:T(8,128)(2,1)S(1)}, bf16[4,24,1792]{2,1,0:T(8,128)(2,1)S(1)}, u32[]{:S(2)}, u32[]{:S(2)}) collective-permute-start(bf16[4,24,1792]{2,1,0:T(8,128)(2,1)S(1)} %slice.18), channel_id=1, source_target_pairs={{0,2},{2,4},{4,6},{6,0},{1,3},{3,5},{5,7},{7,1},{8,10},{10,12},{12... | collective-permute-start | bytes 1032200 | tf_op jit(solution)/shard_map/ppermute | solution.py:271
  69.6 7.7 %collective-permute-start.6 = (bf16[8,24,1792]{2,1,0:T(8,128)(2,1)S(1)}, bf16[8,24,1792]{2,1,0:T(8,128)(2,1)S(1)}, u32[]{:S(2)}, u32[]{:S(2)}) collective-permute-start(bf16[8,24,1792]{2,1,0:T(8,128)(2,1)S(1)} %collective-permute-done.2.refs_3_), channel_id=1, source_target_pairs={{0,1},{1,0},{2,3},{3,2},{4,5},{5,4},{6,7},{7,6},{8,9},{9,8},{10,11... | collective-permute-start | bytes 2064392 | tf_op jit(solution)/shard_map/ppermute | solution.py:274
  77.3 1.9 %collective-permute-start.5 = (bf16[8,24,1792]{2,1,0:T(8,128)(2,1)S(1)}, bf16[8,24,1792]{2,1,0:T(8,128)(2,1)S(1)}, u32[]{:S(2)}, u32[]{:S(2)}) collective-permute-start(bf16[8,24,1792]{2,1,0:T(8,128)(2,1)S(1)} %collective-permute-done.1.refs_2_), channel_id=1, source_target_pairs={{0,1},{1,0},{2,3},{3,2},{4,5},{5,4},{6,7},{7,6},{8,9},{9,8},{10,11... | collective-permute-start | bytes 2064392 | tf_op jit(solution)/shard_map/ppermute | solution.py:274
  79.2 0.0 collective-permute-done.4.refs_5_
  79.2 2.4 %collective-permute-start.8 = (bf16[4,24,1792]{2,1,0:T(8,128)(2,1)S(1)}, bf16[4,24,1792]{2,1,0:T(8,128)(2,1)S(1)}, u32[]{:S(2)}, u32[]{:S(2)}) collective-permute-start(bf16[4,24,1792]{2,1,0:T(8,128)(2,1)S(1)} %collective-permute-done.4.refs_5_), channel_id=1, source_target_pairs={{0,1},{1,0},{2,3},{3,2},{4,5},{5,4},{6,7},{7,6},{8,9},{9,8},{10,11... | collective-permute-start | bytes 1032200 | tf_op jit(solution)/shard_map/ppermute | solution.py:274
  81.7 3.4 %collective-permute-start.7 = (bf16[4,24,1792]{2,1,0:T(8,128)(2,1)S(1)}, bf16[4,24,1792]{2,1,0:T(8,128)(2,1)S(1)}, u32[]{:S(2)}, u32[]{:S(2)}) collective-permute-start(bf16[4,24,1792]{2,1,0:T(8,128)(2,1)S(1)} %collective-permute-done.3.refs_4_), channel_id=1, source_target_pairs={{0,1},{1,0},{2,3},{3,2},{4,5},{5,4},{6,7},{7,6},{8,9},{9,8},{10,11... | collective-permute-start | bytes 1032200 | tf_op jit(solution)/shard_map/ppermute | solution.py:274
  85.1 0.0 collective-permute-done.8.refs_9_
  85.1 1.2 collective-permute-done.7.refs_8_
  86.4 0.7 copy-done.9
  87.1 0.9 copy-done.5
  88.0 6.8 %shard_map.59.yb_ref = f32[1536,256]{1,0:T(8,128)} custom-call(bf16[8,24,1792]{2,1,0:T(8,128)(2,1)} %copy-done, bf16[8,24,1792]{2,1,0:T(8,128)(2,1)} %copy-done.3, bf16[8,24,1792]{2,1,0:T(8,128)(2,1)} %copy-done.2, bf16[8,24,1792]{2,1,0:T(8,128)(2,1)} %copy-done.1, bf16[4,24,1792]{2,1,0:T(8,128)(2,1)} %copy-done.7, bf16[4,24,1792]{2,1,0:T(8,128)(2,1)} %copy-done.6, ...), custom_call_target="tpu_custom_call" | custom-call | flops 1409286144 | bytes 7077888 | tf_op jit(solution)/shard_map/pallas_call | solution.py:60
  94.8 0.0 all-gather.3.cloned.1.call-done.x_ref.a_ref
  94.8 6.6 %shard_map.60 = bf16[768,128]{1,0:T(8,128)(2,1)} custom-call(bf16[1536,2304]{1,0:T(8,128)(2,1)} %all-gather.3.cloned.1.call-done.x_ref.a_ref, bf16[96,8192]{1,0:T(8,128)(2,1)} %bitcast.10, f32[1536,256]{1,0:T(8,128)} %shard_map.59.yb_ref), custom_call_target="tpu_custom_call" | custom-call | tf_op jit(solution)/shard_map/pallas_call | solution.py:95
  101.4 16.5 %all_to_all.21 = bf16[8,96,128]{2,1,0:T(8,128)(2,1)} all-to-all(bf16[8,96,128]{2,1,0:T(8,128)(2,1)} %bitcast.14), channel_id=1, replica_groups=mesh['expert'=8,'z'=8,'x'=4,'c'=2] {'expert'}, dimensions={0} | all-to-all | bytes 393216 | tf_op jit(solution)/shard_map/all_to_all | solution.py:299
  117.9 2.5 %shard_map.61 = (bf16[768,128]{1,0:T(8,128)(2,1)}, f32[1,192]{1,0:T(1,128)}) custom-call(bf16[768,128]{1,0:T(8,128)(2,1)} %bitcast.13, s32[2,192]{1,0:T(2,128)} %bitcast.16, f32[2,192]{1,0:T(2,128)} %bitcast.17), custom_call_target="tpu_custom_call" | custom-call | tf_op jit(solution)/shard_map/pallas_call | solution.py:154
  120.4 7.2 %all-gather = f32[4,1,192]{2,1,0:T(1,128)S(1)} all-gather(f32[1,1,192]{2,1,0:T(1,128)} %bitcast.18), channel_id=1, replica_groups=mesh['expert'=8,'z'=8,'x'=4,'c'=2] {'x'}, dimensions={0}, use_global_device_ids=true | all-gather | bytes 3840 | tf_op jit(solution)/shard_map/all_gather | solution.py:312
  127.7 13.9 %all_to_all.22 = f32[16,1,192]{2,1,0:T(1,128)S(1)} all-to-all(f32[16,1,192]{2,1,0:T(1,128)S(1)} %broadcast_in_dim.8), channel_id=1, replica_groups=mesh['expert'=8,'z'=8,'x'=4,'c'=2] {'z','c'}, dimensions={0} | all-to-all | bytes 24576 | tf_op jit(solution)/shard_map/all_to_all | solution.py:315
  141.5 3.4 %all-to-all-start.2 = ((bf16[8,96,128]{2,1,0:T(8,128)(2,1)}), bf16[8,96,128]{2,1,0:T(8,128)(2,1)S(1)}, u32[]{:S(2)}, u32[]{:S(2)}) async-start(bf16[8,96,128]{2,1,0:T(8,128)(2,1)} %bitcast.15), calls=%async_computation.2 | async-start | bytes 393216 | tf_op jit(solution)/shard_map/all_to_all | solution.py:305
  145.0 0.6 broadcast_multiply_fusion
  145.5 9.2 %all-to-all-done.2 = bf16[8,96,128]{2,1,0:T(8,128)(2,1)S(1)} async-done(((bf16[8,96,128]{2,1,0:T(8,128)(2,1)}), bf16[8,96,128]{2,1,0:T(8,128)(2,1)S(1)}, u32[]{:S(2)}, u32[]{:S(2)}) %all-to-all-start.2) | async-done | bytes 196640 | tf_op jit(solution)/shard_map/all_to_all | solution.py:305
  154.8 0.7 copy-done.10
  155.5 7.7 %shard_map.62 = bf16[96,8192]{1,0:T(8,128)(2,1)} custom-call(bf16[768,128]{1,0:T(8,128)(2,1)} %bitcast.12, bf16[1536,2304]{1,0:T(8,128)(2,1)} %all-gather.3.cloned.1.call-done.x_ref.a_ref, bf16[8,24,1792]{2,1,0:T(8,128)(2,1)} %copy-done, bf16[8,24,1792]{2,1,0:T(8,128)(2,1)} %copy-done.3, bf16[8,24,1792]{2,1,0:T(8,128)(2,1)} %copy-done.2, ...), custom_call_target="tpu_custom_call" | custom-call | flops 2415919104 | bytes 14155776 | tf_op jit(solution)/shard_map/pallas_call | solution.py:234
  (32 shorter events, 0.2 us)
Async XLA Ops:
  7.2 87.6 %all-gather.3.cloned.1.call-start = ((), (), s32[]{:S(2)}) async-start(), calls=%async_computation.4 | async-start | bytes 7520256 | tf_op jit(solution)/shard_map/all_gather | solution.py:268
  48.6 39.3 %copy-start = (bf16[8,24,1792]{2,1,0:T(8,128)(2,1)}, bf16[8,24,1792]{2,1,0:T(8,128)(2,1)S(1)}, u32[]{:S(2)}) copy-start(bf16[8,24,1792]{2,1,0:T(8,128)(2,1)S(1)} %all_to_all.20.refs_0_) | copy-start | bytes 2064388
  48.6 15.6 %collective-permute-start.2 = (bf16[8,24,1792]{2,1,0:T(8,128)(2,1)S(1)}, bf16[8,24,1792]{2,1,0:T(8,128)(2,1)S(1)}, u32[]{:S(2)}, u32[]{:S(2)}) collective-permute-start(bf16[8,24,1792]{2,1,0:T(8,128)(2,1)S(1)} %all_to_all.20.refs_0_), channel_id=1, source_target_pairs={{0,6},{2,0},{4,2},{6,4},{1,7},{3,1},{5,3},{7,5},{8,14},{10,8},{12,... | collective-permute-start | bytes 2064392 | tf_op jit(solution)/shard_map/ppermute | solution.py:271
  50.5 16.9 %collective-permute-start.1 = (bf16[8,24,1792]{2,1,0:T(8,128)(2,1)S(1)}, bf16[8,24,1792]{2,1,0:T(8,128)(2,1)S(1)}, u32[]{:S(2)}, u32[]{:S(2)}) collective-permute-start(bf16[8,24,1792]{2,1,0:T(8,128)(2,1)S(1)} %all_to_all.20.refs_0_), channel_id=1, source_target_pairs={{0,2},{2,4},{4,6},{6,0},{1,3},{3,5},{5,7},{7,1},{8,10},{10,12},{12... | collective-permute-start | bytes 2064392 | tf_op jit(solution)/shard_map/ppermute | solution.py:271
  53.9 31.2 %collective-permute-start = (bf16[8,24,1792]{2,1,0:T(8,128)(2,1)S(1)}, bf16[8,24,1792]{2,1,0:T(8,128)(2,1)S(1)}, u32[]{:S(2)}, u32[]{:S(2)}) collective-permute-start(bf16[8,24,1792]{2,1,0:T(8,128)(2,1)S(1)} %all_to_all.20.refs_0_), channel_id=1, source_target_pairs={{0,1},{1,0},{2,3},{3,2},{4,5},{5,4},{6,7},{7,6},{8,9},{9,8},{10,11... | collective-permute-start | bytes 2064392 | tf_op jit(solution)/shard_map/ppermute | solution.py:274
  64.2 23.7 %copy-start.1 = (bf16[8,24,1792]{2,1,0:T(8,128)(2,1)}, bf16[8,24,1792]{2,1,0:T(8,128)(2,1)S(1)}, u32[]{:S(2)}) copy-start(bf16[8,24,1792]{2,1,0:T(8,128)(2,1)S(1)} %collective-permute-done.2.refs_3_) | copy-start | bytes 2064388
  64.3 15.0 %collective-permute-start.4 = (bf16[4,24,1792]{2,1,0:T(8,128)(2,1)S(1)}, bf16[4,24,1792]{2,1,0:T(8,128)(2,1)S(1)}, u32[]{:S(2)}, u32[]{:S(2)}) collective-permute-start(bf16[4,24,1792]{2,1,0:T(8,128)(2,1)S(1)} %slice.19), channel_id=1, source_target_pairs={{0,6},{2,0},{4,2},{6,4},{1,7},{3,1},{5,3},{7,5},{8,14},{10,8},{12,... | collective-permute-start | bytes 1032200 | tf_op jit(solution)/shard_map/ppermute | solution.py:271
  67.5 20.5 %copy-start.2 = (bf16[8,24,1792]{2,1,0:T(8,128)(2,1)}, bf16[8,24,1792]{2,1,0:T(8,128)(2,1)S(1)}, u32[]{:S(2)}) copy-start(bf16[8,24,1792]{2,1,0:T(8,128)(2,1)S(1)} %collective-permute-done.1.refs_2_) | copy-start | bytes 2064388
  67.5 14.2 %collective-permute-start.3 = (bf16[4,24,1792]{2,1,0:T(8,128)(2,1)S(1)}, bf16[4,24,1792]{2,1,0:T(8,128)(2,1)S(1)}, u32[]{:S(2)}, u32[]{:S(2)}) collective-permute-start(bf16[4,24,1792]{2,1,0:T(8,128)(2,1)S(1)} %slice.18), channel_id=1, source_target_pairs={{0,2},{2,4},{4,6},{6,0},{1,3},{3,5},{5,7},{7,1},{8,10},{10,12},{12... | collective-permute-start | bytes 1032200 | tf_op jit(solution)/shard_map/ppermute | solution.py:271
  69.6 16.7 %collective-permute-start.6 = (bf16[8,24,1792]{2,1,0:T(8,128)(2,1)S(1)}, bf16[8,24,1792]{2,1,0:T(8,128)(2,1)S(1)}, u32[]{:S(2)}, u32[]{:S(2)}) collective-permute-start(bf16[8,24,1792]{2,1,0:T(8,128)(2,1)S(1)} %collective-permute-done.2.refs_3_), channel_id=1, source_target_pairs={{0,1},{1,0},{2,3},{3,2},{4,5},{5,4},{6,7},{7,6},{8,9},{9,8},{10,11... | collective-permute-start | bytes 2064392 | tf_op jit(solution)/shard_map/ppermute | solution.py:274
  77.3 9.0 %collective-permute-start.5 = (bf16[8,24,1792]{2,1,0:T(8,128)(2,1)S(1)}, bf16[8,24,1792]{2,1,0:T(8,128)(2,1)S(1)}, u32[]{:S(2)}, u32[]{:S(2)}) collective-permute-start(bf16[8,24,1792]{2,1,0:T(8,128)(2,1)S(1)} %collective-permute-done.1.refs_2_), channel_id=1, source_target_pairs={{0,1},{1,0},{2,3},{3,2},{4,5},{5,4},{6,7},{7,6},{8,9},{9,8},{10,11... | collective-permute-start | bytes 2064392 | tf_op jit(solution)/shard_map/ppermute | solution.py:274
  79.2 7.1 %copy-start.6 = (bf16[4,24,1792]{2,1,0:T(8,128)(2,1)}, bf16[4,24,1792]{2,1,0:T(8,128)(2,1)S(1)}, u32[]{:S(2)}) copy-start(bf16[4,24,1792]{2,1,0:T(8,128)(2,1)S(1)} %collective-permute-done.4.refs_5_) | copy-start | bytes 1032196
  79.2 5.9 %collective-permute-start.8 = (bf16[4,24,1792]{2,1,0:T(8,128)(2,1)S(1)}, bf16[4,24,1792]{2,1,0:T(8,128)(2,1)S(1)}, u32[]{:S(2)}, u32[]{:S(2)}) collective-permute-start(bf16[4,24,1792]{2,1,0:T(8,128)(2,1)S(1)} %collective-permute-done.4.refs_5_), channel_id=1, source_target_pairs={{0,1},{1,0},{2,3},{3,2},{4,5},{5,4},{6,7},{7,6},{8,9},{9,8},{10,11... | collective-permute-start | bytes 1032200 | tf_op jit(solution)/shard_map/ppermute | solution.py:274
  81.7 4.7 %copy-start.7 = (bf16[4,24,1792]{2,1,0:T(8,128)(2,1)}, bf16[4,24,1792]{2,1,0:T(8,128)(2,1)S(1)}, u32[]{:S(2)}) copy-start(bf16[4,24,1792]{2,1,0:T(8,128)(2,1)S(1)} %collective-permute-done.3.refs_4_) | copy-start | bytes 1032196
  81.7 4.6 %collective-permute-start.7 = (bf16[4,24,1792]{2,1,0:T(8,128)(2,1)S(1)}, bf16[4,24,1792]{2,1,0:T(8,128)(2,1)S(1)}, u32[]{:S(2)}, u32[]{:S(2)}) collective-permute-start(bf16[4,24,1792]{2,1,0:T(8,128)(2,1)S(1)} %collective-permute-done.3.refs_4_), channel_id=1, source_target_pairs={{0,1},{1,0},{2,3},{3,2},{4,5},{5,4},{6,7},{7,6},{8,9},{9,8},{10,11... | collective-permute-start | bytes 1032200 | tf_op jit(solution)/shard_map/ppermute | solution.py:274
  85.1 2.9 %copy-start.3 = (bf16[8,24,1792]{2,1,0:T(8,128)(2,1)}, bf16[8,24,1792]{2,1,0:T(8,128)(2,1)S(1)}, u32[]{:S(2)}) copy-start(bf16[8,24,1792]{2,1,0:T(8,128)(2,1)S(1)} %collective-permute-done.refs_1_) | copy-start | bytes 2064388
  85.1 1.3 copy-start.8
  86.3 0.7 copy-start.9
  86.3 1.6 copy-start.4
  87.1 0.9 copy-start.5
  141.5 13.3 %all-to-all-start.2 = ((bf16[8,96,128]{2,1,0:T(8,128)(2,1)}), bf16[8,96,128]{2,1,0:T(8,128)(2,1)S(1)}, u32[]{:S(2)}, u32[]{:S(2)}) async-start(bf16[8,96,128]{2,1,0:T(8,128)(2,1)} %bitcast.15), calls=%async_computation.2 | async-start | bytes 393216 | tf_op jit(solution)/shard_map/all_to_all | solution.py:305
  154.8 0.7 copy-start.10
Sparse Core Ops, SparseCore 0:
  20.0 64.4 all-gather.2

commit v5 on v4

--- a/solution.py
+++ b/solution.py
@@ -9,7 +9,7 @@
 
 
 LANES = 128
-WIDTH_A, BLOCKS_A, BLOCKS_B = 2304, 2, 2
+WIDTH_A, BLOCKS_A, BLOCKS_B = 2304, 2, 1
 PIECES = 10
 
 
@@ -18,6 +18,24 @@
     pc_ref[...] = jnp.zeros_like(pc_ref)
     pc_ref[0:cols, :] = p_ref[:, start : start + width]
     pc_ref[LANES : LANES + cols, :] = p_ref[:, half + start : half + start + width]
+
+
+def stack_copies(pc_ref, p_ref, start, sem):
+    cols, half, width = p_ref.shape[0], p_ref.shape[1] // 2, pc_ref.shape[1]
+    return [
+        pltpu.make_async_copy(
+            p_ref.at[:, h * half + start : h * half + start + width],
+            pc_ref.at[h * LANES : h * LANES + cols, :],
+            sem.at[h],
+        )
+        for h in range(2)
+    ]
+
+
+def clear_rest(pc_ref, cols):
+    for h in range(2):
+        rest = pc_ref.at[h * LANES + cols : (h + 1) * LANES]
+        rest[...] = jnp.zeros(rest.shape, rest.dtype)
 
 
 def times(x, y):
@@ -40,11 +58,11 @@
 
 
 def forward_b_kernel(start, *refs):
-    pieces, (p_ref, y_ref, pc_ref, all_ref, sem) = refs[:PIECES], refs[PIECES:]
-    copies = piece_copies(pieces, all_ref, sem)
+    pieces, (p_ref, y_ref, pc_ref, all_ref, sem, p_sem) = refs[:PIECES], refs[PIECES:]
+    copies = stack_copies(pc_ref, p_ref, start, p_sem) + piece_copies(pieces, all_ref, sem)
     for copy in copies:
         copy.start()
-    stack_probe(pc_ref, p_ref, start)
+    clear_rest(pc_ref, p_ref.shape[0])
     for copy in copies:
         copy.wait()
     width = pc_ref.shape[1]
@@ -59,14 +77,15 @@
     rows = 1536
     return pl.pallas_call(
         functools.partial(forward_b_kernel, start),
-        in_specs=[pl.BlockSpec(memory_space=pl.ANY)] * PIECES
-        + [pl.BlockSpec(memory_space=pltpu.VMEM)],
+        in_specs=[pl.BlockSpec(memory_space=pltpu.VMEM)] * PIECES
+        + [pl.BlockSpec(memory_space=pl.ANY)],
         out_specs=pl.BlockSpec(memory_space=pltpu.VMEM),
         out_shape=jax.ShapeDtypeStruct((rows, 2 * LANES), jnp.float32),
         scratch_shapes=[
             pltpu.VMEM((2 * LANES, width), jnp.bfloat16),
             pltpu.VMEM((8, 2, 4, 24, width), jnp.bfloat16),
             pltpu.SemaphoreType.DMA((PIECES,)),
+            pltpu.SemaphoreType.DMA((2,)),
         ],
         cost_estimate=pl.CostEstimate(
             flops=2 * rows * width * 2 * LANES,

time: 171 us -> 170 us (level)
  no operation moved by 1% of the time
where the time goes in v5:
time: 170 us; the launch traced here: 169 us
  blocking collectives  77.8 us (46%)
  starting transfers between devices  39.7 us (23%)
  Pallas kernels  22.9 us (13%)
  between operations  14.3 us (8%)
  waiting for transfers between devices  10.5 us (6%)
  local copies, waits for them, and re-layouts  3.44 us (2%)
    all_to_all x1, blocking collectives, gathered(): b = lax.all_to_all(b, 'z', split_axis=0, concat_axis=0, tiled=True)  28.6 us
    ppermute x5, starting transfers between devices, swap(): return lax.ppermute(v, 'c', [(0, 1), (1, 0)])  25.7 us
    all_to_all x1, blocking collectives, local(): lax.all_to_all(tangent.reshape(experts, capacity, LANES), 'expert', split...  16.5 us
    all_to_all x1, blocking collectives, local(): lax.all_to_all(shares, ('z', 'c'), split_axis=0, concat_axis=0, tiled=True)  13.9 us
    all_gather x1, blocking collectives, gathered(): a = lax.all_gather(a, 'x', axis=0, tiled=True)  11.6 us
    ppermute x4, starting transfers between devices, send(): return lax.ppermute(v, 'x', [(i, (i + step) % xs) for i in range(xs)])  10.6 us
    all_to_all x1, waiting for transfers between devices, local(): lax.all_to_all(back.reshape(experts, capacity, LANES), 'expert', split_ax...  9.25 us
    pallas_call x1, Pallas kernels, backward(): pl.pallas_call(functools.partial(backward_kernel, ((n_a, w_a), (n_b, w_b)...  7.32 us
  transfers between devices with their start and end apart: 11, of which 2 were waited for; matrix products, arithmetic and copies ran while one was open for 0% of the time, Pallas kernels for 4%

profile of v5, /device:TPU:1, one launch (start us, length us, event | category | flops | bytes accessed | tf_op | source)
XLA Modules:
  0.0 169.4 jit_solution(14915046172058774610)
XLA Ops:
  7.2 0.0 all-gather.3.cloned.1.call-start
  7.2 1.0 reshape_squeeze.3
  8.3 11.6 %all_gather.9 = bf16[96,2304]{1,0:T(8,128)(2,1)} all-gather(bf16[24,2304]{1,0:T(8,128)(2,1)S(1)} %slice.16), channel_id=1, replica_groups=mesh['expert'=8,'z'=8,'x'=4,'c'=2] {'x'}, dimensions={0}, use_global_device_ids=true | all-gather | bytes 552960 | tf_op jit(solution)/shard_map/all_gather | solution.py:286
  19.9 0.0 all-gather.3.cloned.1.call-update
  20.0 28.6 %all_to_all.20.refs_0_ = bf16[8,24,1792]{2,1,0:T(8,128)(2,1)S(1)} all-to-all(bf16[8,24,1792]{2,1,0:T(8,128)(2,1)S(1)} %broadcast_in_dim.6), channel_id=1, replica_groups=mesh['expert'=8,'z'=8,'x'=4,'c'=2] {'z'}, dimensions={0} | all-to-all | bytes 1376256 | tf_op jit(solution)/shard_map/all_to_all | solution.py:285
  48.6 1.9 %collective-permute-start.2 = (bf16[8,24,1792]{2,1,0:T(8,128)(2,1)S(1)}, bf16[8,24,1792]{2,1,0:T(8,128)(2,1)S(1)}, u32[]{:S(2)}, u32[]{:S(2)}) collective-permute-start(bf16[8,24,1792]{2,1,0:T(8,128)(2,1)S(1)} %all_to_all.20.refs_0_), channel_id=1, source_target_pairs={{0,6},{2,0},{4,2},{6,4},{1,7},{3,1},{5,3},{7,5},{8,14},{10,8},{12,... | collective-permute-start | bytes 2064392 | tf_op jit(solution)/shard_map/ppermute | solution.py:290
  50.5 3.4 %collective-permute-start.1 = (bf16[8,24,1792]{2,1,0:T(8,128)(2,1)S(1)}, bf16[8,24,1792]{2,1,0:T(8,128)(2,1)S(1)}, u32[]{:S(2)}, u32[]{:S(2)}) collective-permute-start(bf16[8,24,1792]{2,1,0:T(8,128)(2,1)S(1)} %all_to_all.20.refs_0_), channel_id=1, source_target_pairs={{0,2},{2,4},{4,6},{6,0},{1,3},{3,5},{5,7},{7,1},{8,10},{10,12},{12... | collective-permute-start | bytes 2064392 | tf_op jit(solution)/shard_map/ppermute | solution.py:290
  53.9 10.3 %collective-permute-start = (bf16[8,24,1792]{2,1,0:T(8,128)(2,1)S(1)}, bf16[8,24,1792]{2,1,0:T(8,128)(2,1)S(1)}, u32[]{:S(2)}, u32[]{:S(2)}) collective-permute-start(bf16[8,24,1792]{2,1,0:T(8,128)(2,1)S(1)} %all_to_all.20.refs_0_), channel_id=1, source_target_pairs={{0,1},{1,0},{2,3},{3,2},{4,5},{5,4},{6,7},{7,6},{8,9},{9,8},{10,11... | collective-permute-start | bytes 2064392 | tf_op jit(solution)/shard_map/ppermute | solution.py:293
  64.2 0.0 collective-permute-done.2.refs_3_
  64.3 3.2 %collective-permute-start.4 = (bf16[4,24,1792]{2,1,0:T(8,128)(2,1)S(1)}, bf16[4,24,1792]{2,1,0:T(8,128)(2,1)S(1)}, u32[]{:S(2)}, u32[]{:S(2)}) collective-permute-start(bf16[4,24,1792]{2,1,0:T(8,128)(2,1)S(1)} %slice.19), channel_id=1, source_target_pairs={{0,6},{2,0},{4,2},{6,4},{1,7},{3,1},{5,3},{7,5},{8,14},{10,8},{12,... | collective-permute-start | bytes 1032200 | tf_op jit(solution)/shard_map/ppermute | solution.py:290
  67.5 2.1 %collective-permute-start.3 = (bf16[4,24,1792]{2,1,0:T(8,128)(2,1)S(1)}, bf16[4,24,1792]{2,1,0:T(8,128)(2,1)S(1)}, u32[]{:S(2)}, u32[]{:S(2)}) collective-permute-start(bf16[4,24,1792]{2,1,0:T(8,128)(2,1)S(1)} %slice.18), channel_id=1, source_target_pairs={{0,2},{2,4},{4,6},{6,0},{1,3},{3,5},{5,7},{7,1},{8,10},{10,12},{12... | collective-permute-start | bytes 1032200 | tf_op jit(solution)/shard_map/ppermute | solution.py:290
  69.6 7.7 %collective-permute-start.6 = (bf16[8,24,1792]{2,1,0:T(8,128)(2,1)S(1)}, bf16[8,24,1792]{2,1,0:T(8,128)(2,1)S(1)}, u32[]{:S(2)}, u32[]{:S(2)}) collective-permute-start(bf16[8,24,1792]{2,1,0:T(8,128)(2,1)S(1)} %collective-permute-done.2.refs_3_), channel_id=1, source_target_pairs={{0,1},{1,0},{2,3},{3,2},{4,5},{5,4},{6,7},{7,6},{8,9},{9,8},{10,11... | collective-permute-start | bytes 2064392 | tf_op jit(solution)/shard_map/ppermute | solution.py:293
  77.3 1.9 %collective-permute-start.5 = (bf16[8,24,1792]{2,1,0:T(8,128)(2,1)S(1)}, bf16[8,24,1792]{2,1,0:T(8,128)(2,1)S(1)}, u32[]{:S(2)}, u32[]{:S(2)}) collective-permute-start(bf16[8,24,1792]{2,1,0:T(8,128)(2,1)S(1)} %collective-permute-done.1.refs_2_), channel_id=1, source_target_pairs={{0,1},{1,0},{2,3},{3,2},{4,5},{5,4},{6,7},{7,6},{8,9},{9,8},{10,11... | collective-permute-start | bytes 2064392 | tf_op jit(solution)/shard_map/ppermute | solution.py:293
  79.2 0.0 collective-permute-done.4.refs_5_
  79.2 2.4 %collective-permute-start.8 = (bf16[4,24,1792]{2,1,0:T(8,128)(2,1)S(1)}, bf16[4,24,1792]{2,1,0:T(8,128)(2,1)S(1)}, u32[]{:S(2)}, u32[]{:S(2)}) collective-permute-start(bf16[4,24,1792]{2,1,0:T(8,128)(2,1)S(1)} %collective-permute-done.4.refs_5_), channel_id=1, source_target_pairs={{0,1},{1,0},{2,3},{3,2},{4,5},{5,4},{6,7},{7,6},{8,9},{9,8},{10,11... | collective-permute-start | bytes 1032200 | tf_op jit(solution)/shard_map/ppermute | solution.py:293
  81.7 3.4 %collective-permute-start.7 = (bf16[4,24,1792]{2,1,0:T(8,128)(2,1)S(1)}, bf16[4,24,1792]{2,1,0:T(8,128)(2,1)S(1)}, u32[]{:S(2)}, u32[]{:S(2)}) collective-permute-start(bf16[4,24,1792]{2,1,0:T(8,128)(2,1)S(1)} %collective-permute-done.3.refs_4_), channel_id=1, source_target_pairs={{0,1},{1,0},{2,3},{3,2},{4,5},{5,4},{6,7},{7,6},{8,9},{9,8},{10,11... | collective-permute-start | bytes 1032200 | tf_op jit(solution)/shard_map/ppermute | solution.py:293
  85.1 0.0 collective-permute-done.8.refs_9_
  85.1 1.2 collective-permute-done.7.refs_8_
  86.4 0.7 copy-done.9
  87.1 0.9 copy-done.5
  88.0 6.5 %shard_map.59.yb_ref = f32[1536,256]{1,0:T(8,128)} custom-call(bf16[8,24,1792]{2,1,0:T(8,128)(2,1)} %copy-done, bf16[8,24,1792]{2,1,0:T(8,128)(2,1)} %copy-done.3, bf16[8,24,1792]{2,1,0:T(8,128)(2,1)} %copy-done.2, bf16[8,24,1792]{2,1,0:T(8,128)(2,1)} %copy-done.1, bf16[4,24,1792]{2,1,0:T(8,128)(2,1)} %copy-done.7, bf16[4,24,1792]{2,1,0:T(8,128)(2,1)} %copy-done.6, ...), custom_call_target="tpu_custom_call" | custom-call | flops 1409286144 | bytes 7077888 | tf_op jit(solution)/shard_map/pallas_call | solution.py:78
  94.5 0.0 all-gather.3.cloned.1.call-done.x_ref.a_ref
  94.5 6.6 %shard_map.60 = bf16[768,128]{1,0:T(8,128)(2,1)} custom-call(bf16[1536,2304]{1,0:T(8,128)(2,1)} %all-gather.3.cloned.1.call-done.x_ref.a_ref, bf16[96,8192]{1,0:T(8,128)(2,1)} %bitcast.10, f32[1536,256]{1,0:T(8,128)} %shard_map.59.yb_ref), custom_call_target="tpu_custom_call" | custom-call | tf_op jit(solution)/shard_map/pallas_call | solution.py:114
  101.1 16.5 %all_to_all.21 = bf16[8,96,128]{2,1,0:T(8,128)(2,1)} all-to-all(bf16[8,96,128]{2,1,0:T(8,128)(2,1)} %bitcast.14), channel_id=1, replica_groups=mesh['expert'=8,'z'=8,'x'=4,'c'=2] {'expert'}, dimensions={0} | all-to-all | bytes 393216 | tf_op jit(solution)/shard_map/all_to_all | solution.py:318
  117.6 2.5 %shard_map.61 = (bf16[768,128]{1,0:T(8,128)(2,1)}, f32[1,192]{1,0:T(1,128)}) custom-call(bf16[768,128]{1,0:T(8,128)(2,1)} %bitcast.13, s32[2,192]{1,0:T(2,128)} %bitcast.16, f32[2,192]{1,0:T(2,128)} %bitcast.17), custom_call_target="tpu_custom_call" | custom-call | tf_op jit(solution)/shard_map/pallas_call | solution.py:173
  120.1 7.2 %all-gather = f32[4,1,192]{2,1,0:T(1,128)S(1)} all-gather(f32[1,1,192]{2,1,0:T(1,128)} %bitcast.18), channel_id=1, replica_groups=mesh['expert'=8,'z'=8,'x'=4,'c'=2] {'x'}, dimensions={0}, use_global_device_ids=true | all-gather | bytes 3840 | tf_op jit(solution)/shard_map/all_gather | solution.py:331
  127.4 13.9 %all_to_all.22 = f32[16,1,192]{2,1,0:T(1,128)S(1)} all-to-all(f32[16,1,192]{2,1,0:T(1,128)S(1)} %broadcast_in_dim.8), channel_id=1, replica_groups=mesh['expert'=8,'z'=8,'x'=4,'c'=2] {'z','c'}, dimensions={0} | all-to-all | bytes 24576 | tf_op jit(solution)/shard_map/all_to_all | solution.py:334
  141.2 3.4 %all-to-all-start.2 = ((bf16[8,96,128]{2,1,0:T(8,128)(2,1)}), bf16[8,96,128]{2,1,0:T(8,128)(2,1)S(1)}, u32[]{:S(2)}, u32[]{:S(2)}) async-start(bf16[8,96,128]{2,1,0:T(8,128)(2,1)} %bitcast.15), calls=%async_computation.2 | async-start | bytes 393216 | tf_op jit(solution)/shard_map/all_to_all | solution.py:324
  144.7 0.6 broadcast_multiply_fusion
  145.2 9.2 %all-to-all-done.2 = bf16[8,96,128]{2,1,0:T(8,128)(2,1)S(1)} async-done(((bf16[8,96,128]{2,1,0:T(8,128)(2,1)}), bf16[8,96,128]{2,1,0:T(8,128)(2,1)S(1)}, u32[]{:S(2)}, u32[]{:S(2)}) %all-to-all-start.2) | async-done | bytes 196640 | tf_op jit(solution)/shard_map/all_to_all | solution.py:324
  154.5 0.7 copy-done.10
  155.2 7.3 %shard_map.62 = bf16[96,8192]{1,0:T(8,128)(2,1)} custom-call(bf16[768,128]{1,0:T(8,128)(2,1)} %bitcast.12, bf16[1536,2304]{1,0:T(8,128)(2,1)} %all-gather.3.cloned.1.call-done.x_ref.a_ref, bf16[8,24,1792]{2,1,0:T(8,128)(2,1)} %copy-done, bf16[8,24,1792]{2,1,0:T(8,128)(2,1)} %copy-done.3, bf16[8,24,1792]{2,1,0:T(8,128)(2,1)} %copy-done.2, ...), custom_call_target="tpu_custom_call" | custom-call | flops 2415919104 | bytes 14155776 | tf_op jit(solution)/shard_map/pallas_call | solution.py:253
  (32 shorter events, 0.2 us)
Async XLA Ops:
  7.2 87.3 %all-gather.3.cloned.1.call-start = ((), (), s32[]{:S(2)}) async-start(), calls=%async_computation.4 | async-start | bytes 7520256 | tf_op jit(solution)/shard_map/all_gather | solution.py:287
  48.6 39.3 %copy-start = (bf16[8,24,1792]{2,1,0:T(8,128)(2,1)}, bf16[8,24,1792]{2,1,0:T(8,128)(2,1)S(1)}, u32[]{:S(2)}) copy-start(bf16[8,24,1792]{2,1,0:T(8,128)(2,1)S(1)} %all_to_all.20.refs_0_) | copy-start | bytes 2064388
  48.6 15.6 %collective-permute-start.2 = (bf16[8,24,1792]{2,1,0:T(8,128)(2,1)S(1)}, bf16[8,24,1792]{2,1,0:T(8,128)(2,1)S(1)}, u32[]{:S(2)}, u32[]{:S(2)}) collective-permute-start(bf16[8,24,1792]{2,1,0:T(8,128)(2,1)S(1)} %all_to_all.20.refs_0_), channel_id=1, source_target_pairs={{0,6},{2,0},{4,2},{6,4},{1,7},{3,1},{5,3},{7,5},{8,14},{10,8},{12,... | collective-permute-start | bytes 2064392 | tf_op jit(solution)/shard_map/ppermute | solution.py:290
  50.5 16.9 %collective-permute-start.1 = (bf16[8,24,1792]{2,1,0:T(8,128)(2,1)S(1)}, bf16[8,24,1792]{2,1,0:T(8,128)(2,1)S(1)}, u32[]{:S(2)}, u32[]{:S(2)}) collective-permute-start(bf16[8,24,1792]{2,1,0:T(8,128)(2,1)S(1)} %all_to_all.20.refs_0_), channel_id=1, source_target_pairs={{0,2},{2,4},{4,6},{6,0},{1,3},{3,5},{5,7},{7,1},{8,10},{10,12},{12... | collective-permute-start | bytes 2064392 | tf_op jit(solution)/shard_map/ppermute | solution.py:290
  53.9 31.2 %collective-permute-start = (bf16[8,24,1792]{2,1,0:T(8,128)(2,1)S(1)}, bf16[8,24,1792]{2,1,0:T(8,128)(2,1)S(1)}, u32[]{:S(2)}, u32[]{:S(2)}) collective-permute-start(bf16[8,24,1792]{2,1,0:T(8,128)(2,1)S(1)} %all_to_all.20.refs_0_), channel_id=1, source_target_pairs={{0,1},{1,0},{2,3},{3,2},{4,5},{5,4},{6,7},{7,6},{8,9},{9,8},{10,11... | collective-permute-start | bytes 2064392 | tf_op jit(solution)/shard_map/ppermute | solution.py:293
  64.2 23.7 %copy-start.1 = (bf16[8,24,1792]{2,1,0:T(8,128)(2,1)}, bf16[8,24,1792]{2,1,0:T(8,128)(2,1)S(1)}, u32[]{:S(2)}) copy-start(bf16[8,24,1792]{2,1,0:T(8,128)(2,1)S(1)} %collective-permute-done.2.refs_3_) | copy-start | bytes 2064388
  64.3 15.0 %collective-permute-start.4 = (bf16[4,24,1792]{2,1,0:T(8,128)(2,1)S(1)}, bf16[4,24,1792]{2,1,0:T(8,128)(2,1)S(1)}, u32[]{:S(2)}, u32[]{:S(2)}) collective-permute-start(bf16[4,24,1792]{2,1,0:T(8,128)(2,1)S(1)} %slice.19), channel_id=1, source_target_pairs={{0,6},{2,0},{4,2},{6,4},{1,7},{3,1},{5,3},{7,5},{8,14},{10,8},{12,... | collective-permute-start | bytes 1032200 | tf_op jit(solution)/shard_map/ppermute | solution.py:290
  67.5 20.5 %copy-start.2 = (bf16[8,24,1792]{2,1,0:T(8,128)(2,1)}, bf16[8,24,1792]{2,1,0:T(8,128)(2,1)S(1)}, u32[]{:S(2)}) copy-start(bf16[8,24,1792]{2,1,0:T(8,128)(2,1)S(1)} %collective-permute-done.1.refs_2_) | copy-start | bytes 2064388
  67.5 14.2 %collective-permute-start.3 = (bf16[4,24,1792]{2,1,0:T(8,128)(2,1)S(1)}, bf16[4,24,1792]{2,1,0:T(8,128)(2,1)S(1)}, u32[]{:S(2)}, u32[]{:S(2)}) collective-permute-start(bf16[4,24,1792]{2,1,0:T(8,128)(2,1)S(1)} %slice.18), channel_id=1, source_target_pairs={{0,2},{2,4},{4,6},{6,0},{1,3},{3,5},{5,7},{7,1},{8,10},{10,12},{12... | collective-permute-start | bytes 1032200 | tf_op jit(solution)/shard_map/ppermute | solution.py:290
  69.6 16.7 %collective-permute-start.6 = (bf16[8,24,1792]{2,1,0:T(8,128)(2,1)S(1)}, bf16[8,24,1792]{2,1,0:T(8,128)(2,1)S(1)}, u32[]{:S(2)}, u32[]{:S(2)}) collective-permute-start(bf16[8,24,1792]{2,1,0:T(8,128)(2,1)S(1)} %collective-permute-done.2.refs_3_), channel_id=1, source_target_pairs={{0,1},{1,0},{2,3},{3,2},{4,5},{5,4},{6,7},{7,6},{8,9},{9,8},{10,11... | collective-permute-start | bytes 2064392 | tf_op jit(solution)/shard_map/ppermute | solution.py:293
  77.3 9.0 %collective-permute-start.5 = (bf16[8,24,1792]{2,1,0:T(8,128)(2,1)S(1)}, bf16[8,24,1792]{2,1,0:T(8,128)(2,1)S(1)}, u32[]{:S(2)}, u32[]{:S(2)}) collective-permute-start(bf16[8,24,1792]{2,1,0:T(8,128)(2,1)S(1)} %collective-permute-done.1.refs_2_), channel_id=1, source_target_pairs={{0,1},{1,0},{2,3},{3,2},{4,5},{5,4},{6,7},{7,6},{8,9},{9,8},{10,11... | collective-permute-start | bytes 2064392 | tf_op jit(solution)/shard_map/ppermute | solution.py:293
  79.2 7.1 %copy-start.6 = (bf16[4,24,1792]{2,1,0:T(8,128)(2,1)}, bf16[4,24,1792]{2,1,0:T(8,128)(2,1)S(1)}, u32[]{:S(2)}) copy-start(bf16[4,24,1792]{2,1,0:T(8,128)(2,1)S(1)} %collective-permute-done.4.refs_5_) | copy-start | bytes 1032196
  79.2 5.9 %collective-permute-start.8 = (bf16[4,24,1792]{2,1,0:T(8,128)(2,1)S(1)}, bf16[4,24,1792]{2,1,0:T(8,128)(2,1)S(1)}, u32[]{:S(2)}, u32[]{:S(2)}) collective-permute-start(bf16[4,24,1792]{2,1,0:T(8,128)(2,1)S(1)} %collective-permute-done.4.refs_5_), channel_id=1, source_target_pairs={{0,1},{1,0},{2,3},{3,2},{4,5},{5,4},{6,7},{7,6},{8,9},{9,8},{10,11... | collective-permute-start | bytes 1032200 | tf_op jit(solution)/shard_map/ppermute | solution.py:293
  81.7 4.7 %copy-start.7 = (bf16[4,24,1792]{2,1,0:T(8,128)(2,1)}, bf16[4,24,1792]{2,1,0:T(8,128)(2,1)S(1)}, u32[]{:S(2)}) copy-start(bf16[4,24,1792]{2,1,0:T(8,128)(2,1)S(1)} %collective-permute-done.3.refs_4_) | copy-start | bytes 1032196
  81.7 4.6 %collective-permute-start.7 = (bf16[4,24,1792]{2,1,0:T(8,128)(2,1)S(1)}, bf16[4,24,1792]{2,1,0:T(8,128)(2,1)S(1)}, u32[]{:S(2)}, u32[]{:S(2)}) collective-permute-start(bf16[4,24,1792]{2,1,0:T(8,128)(2,1)S(1)} %collective-permute-done.3.refs_4_), channel_id=1, source_target_pairs={{0,1},{1,0},{2,3},{3,2},{4,5},{5,4},{6,7},{7,6},{8,9},{9,8},{10,11... | collective-permute-start | bytes 1032200 | tf_op jit(solution)/shard_map/ppermute | solution.py:293
  85.1 2.9 %copy-start.3 = (bf16[8,24,1792]{2,1,0:T(8,128)(2,1)}, bf16[8,24,1792]{2,1,0:T(8,128)(2,1)S(1)}, u32[]{:S(2)}) copy-start(bf16[8,24,1792]{2,1,0:T(8,128)(2,1)S(1)} %collective-permute-done.refs_1_) | copy-start | bytes 2064388
  85.1 1.3 copy-start.8
  86.3 0.7 copy-start.9
  86.3 1.6 copy-start.4
  87.1 0.9 copy-start.5
  141.2 13.3 %all-to-all-start.2 = ((bf16[8,96,128]{2,1,0:T(8,128)(2,1)}), bf16[8,96,128]{2,1,0:T(8,128)(2,1)S(1)}, u32[]{:S(2)}, u32[]{:S(2)}) async-start(bf16[8,96,128]{2,1,0:T(8,128)(2,1)} %bitcast.15), calls=%async_computation.2 | async-start | bytes 393216 | tf_op jit(solution)/shard_map/all_to_all | solution.py:324
  154.5 0.7 copy-start.10
Sparse Core Ops, SparseCore 0:
  20.0 64.4 all-gather.2
